TPU v7x, 32 devices: a whole 2x2x4 slice. The times are simulated.
32 devices in a mesh: replica: 2 (over x), fsdp: 4 (over y, core), ctx: 4 (over z).
Axes of the slice: x: 2, y: 2, z: 4, core: 2. Of those that a mesh axis runs over, the one named last changes fastest.
Arguments:
- hidden_in: bfloat16 [8, 1024, 2048], P(('replica', 'fsdp'), 'ctx'), may hold values from -6 to 6
- teacher: bfloat16 [8, 1024, 2048], P(('replica', 'fsdp'), 'ctx'), may hold values from -6 to 6
- valid_mask: int32 [8, 1024], P(('replica', 'fsdp'), 'ctx'), may hold values from 0 to 1, as said below
- layout: int32 [8, 1024], P(('replica', 'fsdp')), may hold values from 0 to 7, never falling along the last dimension, each value on 1 to 256 neighbouring positions
- routes: int32 [8, 1024, 2], P(('replica', 'fsdp'), 'ctx'), may hold values from 0 to 15, all different within a row; in each aligned block of 256 rows (0 to 255, 256 to 511, ..., all dimensions but the last counted through in order) at most 40 rows name the same one
- attn_gain: bfloat16 [2048], P('fsdp'), may hold values from 0.5 to 1.5
- w_query: bfloat16 [2048, 3072], P('fsdp'), may hold values from -0.125 to 0.125
- w_latent: bfloat16 [2048, 576], P('fsdp'), may hold values from -0.125 to 0.125
- latent_gain: bfloat16 [512], P('fsdp'), may hold values from 0.5 to 1.5
- w_expand: bfloat16 [512, 4096], P('fsdp'), may hold values from -0.25 to 0.25
- w_out: bfloat16 [2048, 2048], P('fsdp'), may hold values from -1.5 to 1.5
- ffn_gain: bfloat16 [2048], P('fsdp'), may hold values from 0.5 to 1.5
- w_router: bfloat16 [2048, 16], P('fsdp'), may hold values from -0.09375 to 0.09375
- shared_gate: bfloat16 [2048, 2816], P('fsdp'), may hold values from -0.125 to 0.125
- shared_up: bfloat16 [2048, 2816], P('fsdp'), may hold values from -0.125 to 0.125
- shared_down: bfloat16 [2816, 2048], P('fsdp'), may hold values from -0.15625 to 0.15625
- expert_gate: bfloat16 [16, 2048, 1408], P(('fsdp', 'ctx'), None, 'replica'), may hold values from -0.125 to 0.125
- expert_up: bfloat16 [16, 2048, 1408], P(('fsdp', 'ctx'), None, 'replica'), may hold values from -0.125 to 0.125
- expert_down: bfloat16 [16, 1408, 2048], P(('fsdp', 'ctx'), 'replica'), may hold values from -0.3125 to 0.3125
Outputs:
- output: bfloat16 [8, 1024, 2048], P(('replica', 'fsdp'), 'ctx')
- loss_value: float32 [], replicated
- input_grad: float32 [8, 1024, 2048], P(('replica', 'fsdp'), 'ctx')
- attn_gain_grad: float32 [2048], P('fsdp')
- w_query_grad: float32 [2048, 3072], P('fsdp')
- w_latent_grad: float32 [2048, 576], P('fsdp')
- latent_gain_grad: float32 [512], P('fsdp')
- w_expand_grad: float32 [512, 4096], P('fsdp')
- w_out_grad: float32 [2048, 2048], P('fsdp')
- ffn_gain_grad: float32 [2048], P('fsdp')
- w_router_grad: float32 [2048, 16], P('fsdp')
- shared_gate_grad: float32 [2048, 2816], P('fsdp')
- shared_up_grad: float32 [2048, 2816], P('fsdp')
- shared_down_grad: float32 [2816, 2048], P('fsdp')
- expert_gate_grad: float32 [16, 2048, 1408], P(('fsdp', 'ctx'), None, 'replica')
- expert_up_grad: float32 [16, 2048, 1408], P(('fsdp', 'ctx'), None, 'replica')
- expert_down_grad: float32 [16, 1408, 2048], P(('fsdp', 'ctx'), 'replica')
Inputs may be any that keep to these rules, and one draw needn't show every extreme that they name: `routes`: each row names 2 different experts; within the rows of one device (aligned blocks of 256 rows) no expert is named more than 40 times. `layout`: within each sequence block numbers start at 0, never fall, and each block holds 1 to 256 positions. `valid_mask`: the first position of every sequence is valid.
All inputs are finite; a program needn't handle non-finite values.
Results may differ from a plain program's by a relative error of at most 0.02.
Values may be sent and summed in bfloat16 or wider, within the bound.
A program may use at most 448 MiB of HBM per device.

v0:
```python
import jax
import jax.numpy as jnp
from jax import lax
from jax.sharding import PartitionSpec as P

D = 2048
HEADS = 16
NOPE = 128
ROPE = 64
VDIM = 128
LATENT = 512


def rms_norm(values, gain_vec):
    return values * lax.rsqrt(jnp.mean(values * values, axis=-1, keepdims=True) + 1e-06) * gain_vec


def rotate(values, cosine, sine_part):
    half_width = values.shape[-1] // 2
    first_half = values[..., :half_width]
    second = values[..., half_width:]
    return jnp.concatenate(
        [first_half * cosine - second * sine_part, first_half * sine_part + second * cosine],
        axis=-1,
    )


def rows_dot(first_mat, second_mat):
    return lax.dot_general(
        first_mat, second_mat, (((0,), (0,)), ((), ())), preferred_element_type=jnp.float32
    )


def cols_dot(first_mat, second_mat):
    return lax.dot_general(
        first_mat, second_mat, (((1,), (1,)), ((), ())), preferred_element_type=jnp.float32
    )


def matmul(first_mat, second_mat):
    return jnp.dot(first_mat, second_mat, preferred_element_type=jnp.float32)


def silu_slope(gate_in, sigmoid_in):
    return sigmoid_in * (1.0 + gate_in * (1.0 - sigmoid_in))


def per_device(
    hidden_in,
    teacher,
    valid_mask,
    layout,
    routes,
    attn_gain,
    w_query,
    w_latent,
    latent_gain,
    w_expand,
    w_out,
    ffn_gain,
    w_router,
    shared_gate,
    shared_up,
    shared_down,
    expert_gate,
    expert_up,
    expert_down,
):
    rep_count = lax.axis_size("replica")
    rows_dev = hidden_in.shape[1]
    offset = lax.axis_index("ctx") * rows_dev
    resid = hidden_in.reshape(rows_dev, D).astype(jnp.float32)
    target = teacher.reshape(rows_dev, D).astype(jnp.float32)
    valid_rows = valid_mask.reshape(rows_dev).astype(jnp.float32)
    key_block = layout[0]
    query_block = lax.dynamic_slice_in_dim(key_block, offset, rows_dev)
    route_ids = routes.reshape(rows_dev, routes.shape[-1])
    top_count = route_ids.shape[1]
    gain_one, query_mat, latent_mat, gain_latent, expand_mat, out_mat = (
        lax.all_gather(attn_gain, "fsdp", axis=0, tiled=True),
        lax.all_gather(w_query, "fsdp", axis=0, tiled=True),
        lax.all_gather(w_latent, "fsdp", axis=0, tiled=True),
        lax.all_gather(latent_gain, "fsdp", axis=0, tiled=True),
        lax.all_gather(w_expand, "fsdp", axis=0, tiled=True),
        lax.all_gather(w_out, "fsdp", axis=0, tiled=True),
    )
    gain_one = gain_one.astype(jnp.float32)
    gain_latent = gain_latent.astype(jnp.float32)
    positions = (offset + jnp.arange(rows_dev)).astype(jnp.float32)
    inverse = 10000.0 ** (-jnp.arange(ROPE // 2, dtype=jnp.float32) * (2.0 / ROPE))
    phase = positions[:, None] * inverse[None, :]
    cosine = jnp.cos(phase)
    sine_part = jnp.sin(phase)

    def turn_query(values):
        return rotate(values, cosine[:, None, :], sine_part[:, None, :])

    def turn_key(values):
        return rotate(values, cosine, sine_part)

    normed = rms_norm(resid, gain_one).astype(jnp.bfloat16)
    query_raw = matmul(normed, query_mat).reshape(rows_dev, HEADS, NOPE + ROPE)
    query_rot = jnp.concatenate(
        [query_raw[..., :NOPE], turn_query(query_raw[..., NOPE:])], axis=-1
    ).astype(jnp.bfloat16)
    latent_raw = matmul(normed, latent_mat)
    latent_part = latent_raw[:, :LATENT]
    rope_part = latent_raw[:, LATENT:]
    latent_own = rms_norm(latent_part, gain_latent).astype(jnp.bfloat16)
    rope_own = turn_key(rope_part).astype(jnp.bfloat16)
    latent_all, rope_all = (
        lax.all_gather(latent_own, "ctx", axis=0, tiled=True),
        lax.all_gather(rope_own, "ctx", axis=0, tiled=True),
    )
    key_count = latent_all.shape[0]
    expanded = (
        matmul(latent_all, expand_mat).astype(jnp.bfloat16).reshape(key_count, HEADS, NOPE + VDIM)
    )
    key_full = jnp.concatenate(
        [expanded[..., :NOPE], jnp.broadcast_to(rope_all[:, None, :], (key_count, HEADS, ROPE))],
        axis=-1,
    )
    value_rows = expanded[..., NOPE:]
    score_scale = (NOPE + ROPE) ** (-0.5)
    allowed = key_block[None, :] <= query_block[:, None]

    def score_rows():
        raw_scores = (
            jnp.einsum("qhd,khd->hqk", query_rot, key_full, preferred_element_type=jnp.float32)
            * score_scale
        )
        return jnp.where(allowed[None], raw_scores, -1e30)

    scores = score_rows()
    peak = jnp.max(scores, axis=-1, keepdims=True)
    log_total = peak + jnp.log(jnp.sum(jnp.exp(scores - peak), axis=-1, keepdims=True))
    attn_probs = jnp.exp(scores - log_total).astype(jnp.bfloat16)
    attended = (
        jnp.einsum("hqk,khv->qhv", attn_probs, value_rows, preferred_element_type=jnp.float32)
        .reshape(rows_dev, HEADS * VDIM)
        .astype(jnp.bfloat16)
    )
    mixed = resid + matmul(attended, out_mat)
    gain_two, router_mat, share_gate_mat, share_up_mat, share_down_mat = (
        lax.all_gather(ffn_gain, "fsdp", axis=0, tiled=True),
        lax.all_gather(w_router, "fsdp", axis=0, tiled=True),
        lax.all_gather(shared_gate, "fsdp", axis=0, tiled=True),
        lax.all_gather(shared_up, "fsdp", axis=0, tiled=True),
        lax.all_gather(shared_down, "fsdp", axis=0, tiled=True),
    )
    gain_two = gain_two.astype(jnp.float32)
    normed_two = rms_norm(mixed, gain_two).astype(jnp.bfloat16)
    logits = matmul(normed_two, router_mat)
    expert_count = logits.shape[1]
    expert_ids = jnp.arange(expert_count, dtype=jnp.int32)
    picks = route_ids[:, :, None] == expert_ids[None, None, :]
    chosen = jnp.sum(jnp.where(picks, logits[:, None, :], 0.0), axis=-1)
    gates = jax.nn.softmax(chosen, axis=-1)
    share_gate_in = matmul(normed_two, share_gate_mat)
    share_up_in = matmul(normed_two, share_up_mat)
    share_sig = jax.nn.sigmoid(share_gate_in)
    share_act = (share_gate_in * share_sig * share_up_in).astype(jnp.bfloat16)
    share_out = matmul(share_act, share_down_mat)
    capacity = 5 * rows_dev * top_count // (4 * expert_count)
    flat_ids = route_ids.reshape(-1)
    hits = (flat_ids[:, None] == expert_ids[None, :]).astype(jnp.int32)
    ranks = jnp.sum((jnp.cumsum(hits, axis=0) - hits) * hits, axis=1)
    slots = flat_ids * capacity + ranks
    pair_rows = jnp.arange(rows_dev * top_count, dtype=jnp.int32)
    owner = (
        jnp.full((expert_count * capacity,), rows_dev, jnp.int32)
        .at[slots]
        .set(pair_rows // top_count)
    )
    padded = jnp.concatenate([normed_two, jnp.zeros((1, D), jnp.bfloat16)], axis=0)
    send_rows = jnp.take(padded, owner, axis=0)
    payload = jnp.broadcast_to(send_rows[None], (rep_count, expert_count * capacity, D)).reshape(
        rep_count * expert_count, capacity, D
    )
    own_gate = expert_gate[0]
    own_up = expert_up[0]
    own_down = expert_down[0]
    arrived = lax.all_to_all(
        payload, ("replica", "fsdp", "ctx"), split_axis=0, concat_axis=0, tiled=True
    )
    source_count, item_count, _ = arrived.shape
    flat_rows = arrived.reshape(source_count * item_count, D)
    gate_in = matmul(flat_rows, own_gate)
    up_in = matmul(flat_rows, own_up)
    act_rows = (gate_in * jax.nn.sigmoid(gate_in) * up_in).astype(jnp.bfloat16)
    partial_out = (
        matmul(act_rows, own_down).astype(jnp.bfloat16).reshape(source_count, item_count, D)
    )
    returned = lax.all_to_all(
        partial_out, ("replica", "fsdp", "ctx"), split_axis=0, concat_axis=0, tiled=True
    )
    returned, received = (returned, arrived)
    slot_out = jnp.sum(
        returned.astype(jnp.float32).reshape(rep_count, expert_count * capacity, D), axis=0
    )
    picked = jnp.take(slot_out, slots, axis=0).reshape(rows_dev, top_count, D)
    final = mixed + share_out + jnp.sum(gates[:, :, None] * picked, axis=1)
    error_rows = final - target
    valid_count, error_total = lax.psum(
        (jnp.sum(valid_rows), jnp.sum(valid_rows[:, None] * error_rows * error_rows)),
        ("replica", "fsdp", "ctx"),
    )
    loss_value = error_total / (valid_count * D)
    grad_final = 2.0 / (valid_count * D) * valid_rows[:, None] * error_rows
    grad_gate = jnp.sum(picked * grad_final[:, None, :], axis=-1)
    grad_chosen = gates * (grad_gate - jnp.sum(gates * grad_gate, axis=-1, keepdims=True))
    grad_logits = jnp.sum(jnp.where(picks, grad_chosen[:, :, None], 0.0), axis=1).astype(
        jnp.bfloat16
    )
    row_grads = (gates[:, :, None] * grad_final[:, None, :]).reshape(rows_dev * top_count, D)
    slot_source = (
        jnp.full((expert_count * capacity,), rows_dev * top_count, jnp.int32)
        .at[slots]
        .set(pair_rows)
    )
    slot_grads = jnp.take(
        jnp.concatenate([row_grads, jnp.zeros((1, D), jnp.float32)], axis=0), slot_source, axis=0
    ).astype(jnp.bfloat16)
    grad_payload = jnp.broadcast_to(
        slot_grads[None], (rep_count, expert_count * capacity, D)
    ).reshape(rep_count * expert_count, capacity, D)
    grad_in = lax.all_to_all(
        grad_payload, ("replica", "fsdp", "ctx"), split_axis=0, concat_axis=0, tiled=True
    )
    rows_flat = received.reshape(-1, D)
    grads_flat = grad_in.reshape(-1, D)
    gate_again = matmul(rows_flat, own_gate)
    up_again = matmul(rows_flat, own_up)
    sigmoid_again = jax.nn.sigmoid(gate_again)
    silu_again = gate_again * sigmoid_again
    act_again = (silu_again * up_again).astype(jnp.bfloat16)
    expert_down_grad = rows_dot(act_again, grads_flat)
    grad_act = cols_dot(grads_flat, own_down)
    grad_gate_in = (grad_act * up_again * silu_slope(gate_again, sigmoid_again)).astype(
        jnp.bfloat16
    )
    grad_up_in = (grad_act * silu_again).astype(jnp.bfloat16)
    expert_gate_grad = rows_dot(rows_flat, grad_gate_in)
    expert_up_grad = rows_dot(rows_flat, grad_up_in)
    grad_rows = (
        (cols_dot(grad_gate_in, own_gate) + cols_dot(grad_up_in, own_up))
        .astype(jnp.bfloat16)
        .reshape(received.shape)
    )
    grad_back = lax.all_to_all(
        grad_rows, ("replica", "fsdp", "ctx"), split_axis=0, concat_axis=0, tiled=True
    )
    grad_slots = jnp.sum(
        grad_back.astype(jnp.float32).reshape(rep_count, expert_count * capacity, D), axis=0
    )
    grad_normed_two = jnp.sum(
        jnp.take(grad_slots, slots, axis=0).reshape(rows_dev, top_count, D), axis=1
    )
    grad_shared = grad_final.astype(jnp.bfloat16)
    full_share_down = rows_dot(share_act, grad_shared)
    grad_share_act = cols_dot(grad_shared, share_down_mat)
    grad_share_gate = (grad_share_act * share_up_in * silu_slope(share_gate_in, share_sig)).astype(
        jnp.bfloat16
    )
    grad_share_up = (grad_share_act * share_gate_in * share_sig).astype(jnp.bfloat16)
    full_share_gate = rows_dot(normed_two, grad_share_gate)
    full_share_up = rows_dot(normed_two, grad_share_up)
    full_router = rows_dot(normed_two, grad_logits)
    grad_normed_two = (
        grad_normed_two
        + cols_dot(grad_share_gate, share_gate_mat)
        + cols_dot(grad_share_up, share_up_mat)
        + cols_dot(grad_logits, router_mat)
    )
    _, norm_two_back = jax.vjp(rms_norm, mixed, gain_two)
    grad_mixed_norm, gain_two_grad = norm_two_back(grad_normed_two)
    grad_mixed = grad_final + grad_mixed_norm
    grad_mix = grad_mixed.astype(jnp.bfloat16)
    full_out = rows_dot(attended, grad_mix)
    grad_att = cols_dot(grad_mix, out_mat).astype(jnp.bfloat16).reshape(rows_dev, HEADS, VDIM)
    scores = score_rows()
    prob_rows = jnp.exp(scores - log_total)
    prob_low = prob_rows.astype(jnp.bfloat16)
    grad_value = jnp.einsum("hqk,qhv->khv", prob_low, grad_att, preferred_element_type=jnp.float32)
    grad_probs = jnp.einsum(
        "qhv,khv->hqk", grad_att, value_rows, preferred_element_type=jnp.float32
    )
    row_dot = jnp.sum(prob_rows * grad_probs, axis=-1, keepdims=True)
    grad_scores = (prob_rows * (grad_probs - row_dot)).astype(jnp.bfloat16)
    grad_query = (
        jnp.einsum("hqk,khd->qhd", grad_scores, key_full, preferred_element_type=jnp.float32)
        * score_scale
    )
    grad_key = (
        jnp.einsum("hqk,qhd->khd", grad_scores, query_rot, preferred_element_type=jnp.float32)
        * score_scale
    )
    grad_expanded = (
        jnp.concatenate([grad_key[..., :NOPE], grad_value], axis=-1)
        .astype(jnp.bfloat16)
        .reshape(key_count, HEADS * (NOPE + VDIM))
    )
    full_expand = rows_dot(latent_all, grad_expanded)
    grad_latent_all = cols_dot(grad_expanded, expand_mat)
    grad_rope_all = jnp.sum(grad_key[..., NOPE:], axis=1)
    grad_latent_own, grad_rope_own = (
        lax.psum_scatter(
            grad_latent_all.astype(jnp.bfloat16), "ctx", scatter_dimension=0, tiled=True
        ).astype(jnp.float32),
        lax.psum_scatter(
            grad_rope_all.astype(jnp.bfloat16), "ctx", scatter_dimension=0, tiled=True
        ).astype(jnp.float32),
    )
    _, latent_back = jax.vjp(rms_norm, latent_part, gain_latent)
    grad_latent_part, gain_latent_grad = latent_back(grad_latent_own)
    _, rope_back = jax.vjp(turn_key, rope_part)
    (grad_rope_raw,) = rope_back(grad_rope_own)
    grad_latent_raw = jnp.concatenate([grad_latent_part, grad_rope_raw], axis=-1).astype(
        jnp.bfloat16
    )
    _, query_back = jax.vjp(turn_query, query_raw[..., NOPE:])
    (grad_query_rope,) = query_back(grad_query[..., NOPE:])
    grad_query_raw = (
        jnp.concatenate([grad_query[..., :NOPE], grad_query_rope], axis=-1)
        .astype(jnp.bfloat16)
        .reshape(rows_dev, HEADS * (NOPE + ROPE))
    )
    full_query = rows_dot(normed, grad_query_raw)
    full_latent = rows_dot(normed, grad_latent_raw)
    grad_normed = cols_dot(grad_query_raw, query_mat) + cols_dot(grad_latent_raw, latent_mat)
    _, norm_one_back = jax.vjp(rms_norm, resid, gain_one)
    grad_resid_norm, gain_one_grad = norm_one_back(grad_normed)
    input_grad = grad_mixed + grad_resid_norm
    (
        g_gain_one,
        g_query,
        g_latent,
        g_gain_latent,
        g_expand,
        g_out,
        g_gain_two,
        g_router,
        g_share_gate,
        g_share_up,
        g_share_down,
    ) = (
        lax.psum_scatter(
            gain_one_grad.astype(jnp.bfloat16), "fsdp", scatter_dimension=0, tiled=True
        ).astype(jnp.float32),
        lax.psum_scatter(
            full_query.astype(jnp.bfloat16), "fsdp", scatter_dimension=0, tiled=True
        ).astype(jnp.float32),
        lax.psum_scatter(
            full_latent.astype(jnp.bfloat16), "fsdp", scatter_dimension=0, tiled=True
        ).astype(jnp.float32),
        lax.psum_scatter(
            gain_latent_grad.astype(jnp.bfloat16), "fsdp", scatter_dimension=0, tiled=True
        ).astype(jnp.float32),
        lax.psum_scatter(
            full_expand.astype(jnp.bfloat16), "fsdp", scatter_dimension=0, tiled=True
        ).astype(jnp.float32),
        lax.psum_scatter(
            full_out.astype(jnp.bfloat16), "fsdp", scatter_dimension=0, tiled=True
        ).astype(jnp.float32),
        lax.psum_scatter(
            gain_two_grad.astype(jnp.bfloat16), "fsdp", scatter_dimension=0, tiled=True
        ).astype(jnp.float32),
        lax.psum_scatter(
            full_router.astype(jnp.bfloat16), "fsdp", scatter_dimension=0, tiled=True
        ).astype(jnp.float32),
        lax.psum_scatter(
            full_share_gate.astype(jnp.bfloat16), "fsdp", scatter_dimension=0, tiled=True
        ).astype(jnp.float32),
        lax.psum_scatter(
            full_share_up.astype(jnp.bfloat16), "fsdp", scatter_dimension=0, tiled=True
        ).astype(jnp.float32),
        lax.psum_scatter(
            full_share_down.astype(jnp.bfloat16), "fsdp", scatter_dimension=0, tiled=True
        ).astype(jnp.float32),
    )
    (
        g_gain_one,
        g_query,
        g_latent,
        g_gain_latent,
        g_expand,
        g_out,
        g_gain_two,
        g_router,
        g_share_gate,
        g_share_up,
        g_share_down,
    ) = (
        lax.psum(g_gain_one.astype(jnp.bfloat16), ("replica", "ctx")).astype(jnp.float32),
        lax.psum(g_query.astype(jnp.bfloat16), ("replica", "ctx")).astype(jnp.float32),
        lax.psum(g_latent.astype(jnp.bfloat16), ("replica", "ctx")).astype(jnp.float32),
        lax.psum(g_gain_latent.astype(jnp.bfloat16), ("replica", "ctx")).astype(jnp.float32),
        lax.psum(g_expand.astype(jnp.bfloat16), ("replica", "ctx")).astype(jnp.float32),
        lax.psum(g_out.astype(jnp.bfloat16), ("replica", "ctx")).astype(jnp.float32),
        lax.psum(g_gain_two.astype(jnp.bfloat16), ("replica", "ctx")).astype(jnp.float32),
        lax.psum(g_router.astype(jnp.bfloat16), ("replica", "ctx")).astype(jnp.float32),
        lax.psum(g_share_gate.astype(jnp.bfloat16), ("replica", "ctx")).astype(jnp.float32),
        lax.psum(g_share_up.astype(jnp.bfloat16), ("replica", "ctx")).astype(jnp.float32),
        lax.psum(g_share_down.astype(jnp.bfloat16), ("replica", "ctx")).astype(jnp.float32),
    )
    return (
        final.astype(jnp.bfloat16).reshape(1, rows_dev, D),
        loss_value,
        input_grad.reshape(1, rows_dev, D),
        g_gain_one,
        g_query,
        g_latent,
        g_gain_latent,
        g_expand,
        g_out,
        g_gain_two,
        g_router,
        g_share_gate,
        g_share_up,
        g_share_down,
        expert_gate_grad[None],
        expert_up_grad[None],
        expert_down_grad[None],
    )


def solution(mesh):
    return jax.shard_map(
        per_device,
        mesh=mesh,
        in_specs=(
            P(("replica", "fsdp"), "ctx", None),
            P(("replica", "fsdp"), "ctx", None),
            P(("replica", "fsdp"), "ctx"),
            P(("replica", "fsdp"), None),
            P(("replica", "fsdp"), "ctx", None),
            P("fsdp"),
            P("fsdp", None),
            P("fsdp", None),
            P("fsdp"),
            P("fsdp", None),
            P("fsdp", None),
            P("fsdp"),
            P("fsdp", None),
            P("fsdp", None),
            P("fsdp", None),
            P("fsdp", None),
            P(("fsdp", "ctx"), None, "replica"),
            P(("fsdp", "ctx"), None, "replica"),
            P(("fsdp", "ctx"), "replica", None),
        ),
        out_specs=(
            P(("replica", "fsdp"), "ctx", None),
            P(),
            P(("replica", "fsdp"), "ctx", None),
            P("fsdp"),
            P("fsdp", None),
            P("fsdp", None),
            P("fsdp"),
            P("fsdp", None),
            P("fsdp", None),
            P("fsdp"),
            P("fsdp", None),
            P("fsdp", None),
            P("fsdp", None),
            P("fsdp", None),
            P(("fsdp", "ctx"), None, "replica"),
            P(("fsdp", "ctx"), None, "replica"),
            P(("fsdp", "ctx"), "replica", None),
        ),
        check_vma=False,
    )
```

profile of v0, /device:TPU:0, one launch (start us, length us, event | category | flops | bytes accessed | tf_op | source)
XLA Modules:
  0.0 2167.8 jit_solution(8107467943738031104)
XLA Ops:
  8.7 6.2 all-gather.1
  22.5 14.0 all-gather.12.cloned.1.call-done
  66.9 13.4 all_gather.45
  80.3 26.3 %all-gather.16.cloned.1.call-done = bf16[512,4096]{1,0:T(8,128)(2,1)} async-done(((bf16[128,4096]{1,0:T(8,128)(2,1)}), bf16[512,4096]{1,0:T(8,128)(2,1)}) %all-gather.16.cloned.1.call-update) | async-done | bytes 4194320 | tf_op jit(solution)/shard_map/all_gather | solution.py:84
  106.6 11.3 convolution_convert_fusion.6
  118.0 11.8 copy.88
  134.7 55.5 %all-gather.18.cloned.1.call-done = bf16[2048,3072]{1,0:T(8,128)(2,1)} async-done(((bf16[512,3072]{1,0:T(8,128)(2,1)}), bf16[2048,3072]{1,0:T(8,128)(2,1)}) %all-gather.18.cloned.1.call-update) | async-done | bytes 12582928 | tf_op jit(solution)/shard_map/all_gather | solution.py:81
  190.2 16.5 copy.72
  206.7 7.0 fusion.41
  216.6 10.6 fusion
  227.2 8.2 exponential_reduce_fusion
  236.0 8.8 fusion.37
  249.9 6.4 multiply_reduce_fusion.5
  259.9 8.7 gather_fusion
  279.2 111.6 %all-to-all-done = bf16[32,40,2048]{2,1,0:T(8,128)(2,1)} async-done(((bf16[32,40,2048]{2,1,0:T(8,128)(2,1)}), bf16[32,40,2048]{2,1,0:T(8,128)(2,1)}, u32[]{:S(2)}, u32[]{:S(2)}) %all-to-all-start) | async-done | bytes 5242912 | tf_op jit(solution)/shard_map/all_to_all | solution.py:183
  390.8 9.0 fusion.17
  399.8 9.7 multiply_convert_fusion.3
  415.6 7.8 all-to-all-start.1
  426.1 44.9 %all_gather.51 = bf16[2048,16]{0,1:T(8,128)(2,1)S(1)} all-gather(bf16[512,16]{0,1:T(8,128)(2,1)S(1)} %copy-done.57), channel_id=1, replica_groups=mesh['replica'=2,'fsdp'=4,'ctx'=4] {'fsdp'}, dimensions={0}, use_global_device_ids=true | all-gather | bytes 81920 | tf_op jit(solution)/shard_map/all_gather | solution.py:146
  473.7 9.3 fusion.102
  483.0 20.9 all-gather.24.cloned.1.call-done
  503.9 10.7 multiply_convert_fusion.6
  514.6 21.2 all-to-all-done.1
  535.8 6.6 convert_reduce_fusion.1
  542.4 7.9 gather_fusion.2
  560.8 10.1 multiply_reduce_fusion.2
  571.0 17.9 all-gather.26.cloned.1.call-done
  588.9 11.4 fusion.33
  600.2 40.5 %all-reduce.9 = (f32[]{:T(128)}, f32[]{:T(128)}) all-reduce(f32[]{:T(128)} %get-tuple-element.68, f32[]{:T(128)} %convert_reduce_fusion.2), channel_id=1, replica_groups=mesh['replica'=2,'fsdp'=4,'ctx'=4] {'replica','fsdp','ctx'}, use_global_device_ids=true, to_apply=%region_15.17 | all-reduce | flops 2 | bytes 16 | tf_op jit(solution)/shard_map/psum | solution.py:204
  661.0 8.8 gather_fusion.1
  672.8 120.8 %all_to_all.20 = bf16[32,40,2048]{2,1,0:T(8,128)(2,1)S(1)} all-to-all(bf16[32,40,2048]{2,1,0:T(8,128)(2,1)S(1)} %bitcast.192), channel_id=1, replica_groups=mesh['replica'=2,'fsdp'=4,'ctx'=4] {'replica','fsdp','ctx'}, dimensions={0} | all-to-all | bytes 10485760 | tf_op jit(solution)/shard_map/all_to_all | solution.py:227
  803.1 6.2 add_convert_fusion
  818.5 11.6 multiply_convert_fusion.4
  830.1 96.0 %all-to-all-done.3 = bf16[32,40,2048]{2,1,0:T(8,128)(2,1)} async-done(((bf16[32,40,2048]{2,1,0:T(8,128)(2,1)}), bf16[32,40,2048]{2,1,0:T(8,128)(2,1)}, u32[]{:S(2)}, u32[]{:S(2)}) %all-to-all-start.3) | async-done | bytes 5242912 | tf_op jit(solution)/shard_map/all_to_all | solution.py:250
  926.2 6.6 convert_reduce_fusion
  932.8 7.9 gather_fusion.3
  951.2 7.2 reduce_sum.269
  958.4 9.3 convolution_add_fusion.3
  967.8 8.2 convolution_add_fusion.2
  982.9 9.6 convert_bitcast_fusion
  992.5 14.3 multiply_reduce_fusion
  1006.8 12.5 multiply_convert_fusion
  1034.4 8.0 pad_maximum_fusion
  1042.4 10.3 convolution_convert_fusion.11
  1052.8 7.3 convolution_convert_fusion.2
  1076.3 8.5 reduce-scatter.11.cloned.1.call-done
  1089.8 12.0 convolution_convert_fusion.7
  1102.0 7.9 convolution_convert_fusion.4
  1110.0 10.8 multiply_bitcast_fusion.1
  1125.2 6.7 convolution_convert_fusion.3
  1133.1 45.1 %reduce-scatter.29.cloned.1.call-done = bf16[704,2048]{1,0:T(8,128)(2,1)} async-done(((bf16[2816,2048]{1,0:T(8,128)(2,1)}), bf16[704,2048]{1,0:T(8,128)(2,1)}) %reduce-scatter.29.cloned.1.call-update) | async-done | bytes 2883600 | tf_op jit(solution)/shard_map/reduce_scatter | solution.py:377
  1178.3 94.7 %reduce-scatter.27.cloned.1.call-done = bf16[512,2816]{1,0:T(8,128)(2,1)} async-done(((bf16[2048,2816]{1,0:T(8,128)(2,1)}), bf16[512,2816]{1,0:T(8,128)(2,1)}) %reduce-scatter.27.cloned.1.call-update) | async-done | bytes 2883600 | tf_op jit(solution)/shard_map/reduce_scatter | solution.py:374
  1273.0 94.8 %reduce-scatter.25.cloned.1.call-done = bf16[512,2816]{1,0:T(8,128)(2,1)} async-done(((bf16[2048,2816]{1,0:T(8,128)(2,1)}), bf16[512,2816]{1,0:T(8,128)(2,1)}) %reduce-scatter.25.cloned.1.call-update) | async-done | bytes 2883600 | tf_op jit(solution)/shard_map/reduce_scatter | solution.py:371
  1367.8 36.1 %reduce-scatter.17.cloned.1.call-done = bf16[512,576]{0,1:T(8,128)(2,1)} async-done(((bf16[2048,576]{0,1:T(8,128)(2,1)}), bf16[512,576]{0,1:T(8,128)(2,1)}) %reduce-scatter.17.cloned.1.call-update) | async-done | bytes 589840 | tf_op jit(solution)/shard_map/reduce_scatter | solution.py:353
  1403.8 47.7 %reduce-scatter.19.cloned.1.call-done = bf16[128,4096]{1,0:T(8,128)(2,1)} async-done(((bf16[512,4096]{1,0:T(8,128)(2,1)}), bf16[128,4096]{1,0:T(8,128)(2,1)}) %reduce-scatter.19.cloned.1.call-update) | async-done | bytes 1048592 | tf_op jit(solution)/shard_map/reduce_scatter | solution.py:359
  1451.5 74.2 %reduce-scatter.21.cloned.1.call-done = bf16[512,2048]{1,0:T(8,128)(2,1)} async-done(((bf16[2048,2048]{1,0:T(8,128)(2,1)}), bf16[512,2048]{1,0:T(8,128)(2,1)}) %reduce-scatter.21.cloned.1.call-update) | async-done | bytes 2097168 | tf_op jit(solution)/shard_map/reduce_scatter | solution.py:362
  1525.7 101.7 %reduce-scatter.15.cloned.1.call-done = bf16[512,3072]{1,0:T(8,128)(2,1)} async-done(((bf16[2048,3072]{1,0:T(8,128)(2,1)}), bf16[512,3072]{1,0:T(8,128)(2,1)}) %reduce-scatter.15.cloned.1.call-update) | async-done | bytes 3145744 | tf_op jit(solution)/shard_map/reduce_scatter | solution.py:350
  1630.6 9.6 convolution_bitcast_fusion.2
  1640.2 8.3 convolution_bitcast_fusion
  1648.4 8.3 convolution_bitcast_fusion.1
  1656.7 6.9 fusion.104
  1666.3 6.3 all-reduce.12
  1672.8 40.3 %all-reduce.10 = (bf16[512]{0:T(512)(128)(2,1)S(1)}, bf16[128]{0:T(256)(128)(2,1)S(1)}, bf16[512]{0:T(512)(128)(2,1)S(1)}, bf16[512,16]{0,1:T(8,128)(2,1)S(1)}) all-reduce(bf16[512]{0:T(512)(128)(2,1)S(1)} %dynamic-slice.2, bf16[128]{0:T(256)(128)(2,1)S(1)} %dynamic-slice.4, ...), channel_id=1, replica_groups=mesh['replica'=2,'fsdp'=4,'ctx'=4] {'replica','ctx'}, use_global_device_ids=true, to_apply=%region_33.35 | all-reduce | flops 9344 | bytes 37376 | tf_op jit(solution)/shard_map/psum | solution.py:394
  1719.5 419.7 %all-reduce.15.cloned.1.call-done = (bf16[512,3072]{1,0:T(8,128)(2,1)}, bf16[512,576]{0,1:T(8,128)(2,1)}, bf16[128,4096]{1,0:T(8,128)(2,1)}, bf16[512,2048]{1,0:...) async-done(((bf16[512,3072]{1,0:T(8,128)(2,1)}, bf16[512,576]{0,1:T(8,128)(2,1)}, bf16[128,4096]{1,0:T(8,128)(2,1)}, ...) | async-done | bytes 15532048 | tf_op jit(solution)/shard_map/psum | solution.py:395
  (353 shorter events, 220.1 us)
Async XLA Ops:
  7.2 402.4 %copy-start = (bf16[1,704,2048]{2,1,0:T(8,128)(2,1)S(1)}, bf16[1,704,2048]{2,1,0:T(8,128)(2,1)}, u32[]{:S(2)}) copy-start(bf16[1,704,2048]{2,1,0:T(8,128)(2,1)} %param.39) | copy-start | bytes 8650756
  7.2 29.2 %all-gather.12.cloned.1.call-start = ((), (), s32[]{:S(2)}) async-start(), calls=%async_computation.14 | async-start | bytes 2949120 | tf_op jit(solution)/shard_map/all_gather | solution.py:82
  7.9 72.4 %all-gather.14.cloned.1.call-start = ((), (), s32[]{:S(2)}) async-start(), calls=%async_computation.15 | async-start | bytes 1310720 | tf_op jit(solution)/shard_map/all_gather | solution.py:112
  14.9 25.1 %copy-start.48 = (f32[4,1,128]{2,1,0:T(1,128)}, f32[4,1,128]{2,1,0:T(1,128)S(1)}, u32[]{:S(2)}) copy-start(f32[4,1,128]{2,1,0:T(1,128)S(1)} %convert_element_type.327) | copy-start | bytes 6148
  20.3 186.4 %copy-start.35 = (f32[4,1,512]{2,1,0:T(1,128)}, f32[4,1,512]{2,1,0:T(1,128)S(1)}, u32[]{:S(2)}) copy-start(f32[4,1,512]{2,1,0:T(1,128)S(1)} %convert_element_type.326) | copy-start | bytes 24580
  22.4 19.0 copy-start.45
  39.3 26.7 %copy-start.14 = (f32[256,576]{0,1:T(8,128)}, f32[256,576]{0,1:T(8,128)S(1)}, u32[]{:S(2)}) copy-start(f32[256,576]{0,1:T(8,128)S(1)} %fusion.57) | copy-start | bytes 1769476
  41.5 65.1 %all-gather.16.cloned.1.call-start = ((), (), s32[]{:S(2)}) async-start(), calls=%async_computation.16 | async-start | bytes 5242880 | tf_op jit(solution)/shard_map/all_gather | solution.py:84
  42.2 148.0 %all-gather.18.cloned.1.call-start = ((), (), s32[]{:S(2)}) async-start(), calls=%async_computation.17 | async-start | bytes 15728640 | tf_op jit(solution)/shard_map/all_gather | solution.py:81
  42.8 207.1 %all-gather.20.cloned.1.call-start = ((), (), s32[]{:S(2)}) async-start(), calls=%async_computation.18 | async-start | bytes 10485760 | tf_op jit(solution)/shard_map/all_gather | solution.py:85
  43.4 430.3 %all-gather.22.cloned.1.call-start = ((), (), s32[]{:S(2)}) async-start(), calls=%async_computation.19 | async-start | bytes 14417920 | tf_op jit(solution)/shard_map/all_gather | solution.py:147
  44.0 459.9 %all-gather.24.cloned.1.call-start = ((), (), s32[]{:S(2)}) async-start(), calls=%async_computation.20 | async-start | bytes 14417920 | tf_op jit(solution)/shard_map/all_gather | solution.py:148
  54.6 201.8 %copy-start.43 = (f32[4,1,512]{2,1,0:T(1,128)}, f32[4,1,512]{2,1,0:T(1,128)S(1)}, u32[]{:S(2)}) copy-start(f32[4,1,512]{2,1,0:T(1,128)S(1)} %convert_element_type.328) | copy-start | bytes 24580
  66.9 147.0 %copy-start.37 = (f32[256,32]{0,1:T(8,128)}, f32[256,32]{0,1:T(8,128)S(1)}, u32[]{:S(2)}) copy-start(f32[256,32]{0,1:T(8,128)S(1)} %get-tuple-element.56) | copy-start | bytes 98308
  66.9 147.0 %copy-start.39 = (f32[256,32]{0,1:T(8,128)}, f32[256,32]{0,1:T(8,128)S(1)}, u32[]{:S(2)}) copy-start(f32[256,32]{0,1:T(8,128)S(1)} %get-tuple-element.57) | copy-start | bytes 98308
  190.2 16.5 copy-start.46
  213.9 13.4 copy-start.21
  215.0 12.2 copy-start.32
  215.0 21.0 slice-start
  216.6 19.4 slice-start.1
  256.3 12.4 copy-start.66
  256.3 12.3 copy-start.60
  259.9 8.8 copy-start.69
  273.7 117.1 %all-to-all-start = ((bf16[32,40,2048]{2,1,0:T(8,128)(2,1)}), bf16[32,40,2048]{2,1,0:T(8,128)(2,1)}, u32[]{:S(2)}, u32[]{:S(2)}) async-start(bf16[32,40,2048]{2,1,0:T(8,128)(2,1)} %bitcast.191), calls=%async_computation | async-start | bytes 10485760 | tf_op jit(solution)/shard_map/all_to_all | solution.py:183
  278.4 310.5 %all-gather.26.cloned.1.call-start = ((), (), s32[]{:S(2)}) async-start(), calls=%async_computation.21 | async-start | bytes 14417920 | tf_op jit(solution)/shard_map/all_gather | solution.py:149
  390.8 9.0 copy-start.76
  399.8 9.8 copy-start.84
  415.6 10.5 copy-start.57
  415.6 55.4 %copy-start.52 = (s32[512]{0:T(512)S(1)}, s32[512]{0:T(512)}, u32[]{:S(2)}) copy-start(s32[512]{0:T(512)} %eq.44) | copy-start | bytes 6148
  415.6 55.4 %copy-start.54 = (s32[512]{0:T(512)S(1)}, s32[512]{0:T(512)}, u32[]{:S(2)}) copy-start(s32[512]{0:T(512)} %copy-done.53) | copy-start | bytes 6148
  415.6 57.7 %copy-start.51 = (s32[1,256,2]{1,2,0:T(2,128)S(1)}, s32[1,256,2]{1,2,0:T(2,128)}, u32[]{:S(2)}) copy-start(s32[1,256,2]{1,2,0:T(2,128)} %param.25) | copy-start | bytes 6148
  415.6 120.2 %all-to-all-start.1 = ((bf16[32,40,2048]{2,1,0:T(8,128)(2,1)}), bf16[32,40,2048]{2,1,0:T(8,128)(2,1)}, u32[]{:S(2)}, u32[]{:S(2)}) async-start(bf16[32,40,2048]{2,1,0:T(8,128)(2,1)} %bitcast.205), calls=%async_computation.1 | async-start | bytes 10485760 | tf_op jit(solution)/shard_map/all_to_all | solution.py:194
  672.8 120.9 %copy-start.85 = (f32[1280,704]{0,1:T(8,128)S(1)}, f32[1280,704]{0,1:T(8,128)}, u32[]{:S(2)}) copy-start(f32[1280,704]{0,1:T(8,128)} %copy-done.84) | copy-start | bytes 10813444
  672.8 120.9 %copy-start.86 = (f32[1280,704]{0,1:T(8,128)S(1)}, f32[1280,704]{0,1:T(8,128)}, u32[]{:S(2)}) copy-start(f32[1280,704]{0,1:T(8,128)} %get-tuple-element.65) | copy-start | bytes 10813444
  809.3 116.9 %all-to-all-start.3 = ((bf16[32,40,2048]{2,1,0:T(8,128)(2,1)}), bf16[32,40,2048]{2,1,0:T(8,128)(2,1)}, u32[]{:S(2)}, u32[]{:S(2)}) async-start(bf16[32,40,2048]{2,1,0:T(8,128)(2,1)} %bitcast.206), calls=%async_computation.3 | async-start | bytes 10485760 | tf_op jit(solution)/shard_map/all_to_all | solution.py:250
  813.9 261.4 %reduce-scatter.13.cloned.1.call-start = ((), (), s32[]{:S(2)}) async-start(), calls=%async_computation.23 | async-start | bytes 163840 | tf_op jit(solution)/shard_map/reduce_scatter | solution.py:310
  958.4 9.4 copy-start.30
  958.4 21.0 slice-start.2
  967.8 11.7 slice-start.3
  1006.8 12.5 copy-start.22
  1006.8 12.5 copy-start.33
  1006.8 12.5 copy-start.34
  1034.1 50.7 %reduce-scatter.11.cloned.1.call-start = ((), (), s32[]{:S(2)}) async-start(), calls=%async_computation.22 | async-start | bytes 1310720 | tf_op jit(solution)/shard_map/reduce_scatter | solution.py:307
  1042.4 10.4 copy-start.12
  1052.7 125.6 %reduce-scatter.29.cloned.1.call-start = ((), (), s32[]{:S(2)}) async-start(), calls=%async_computation.31 | async-start | bytes 14417920 | tf_op jit(solution)/shard_map/reduce_scatter | solution.py:377
  1060.1 212.8 %reduce-scatter.27.cloned.1.call-start = ((), (), s32[]{:S(2)}) async-start(), calls=%async_computation.30 | async-start | bytes 14417920 | tf_op jit(solution)/shard_map/reduce_scatter | solution.py:374
  1067.7 300.0 %reduce-scatter.25.cloned.1.call-start = ((), (), s32[]{:S(2)}) async-start(), calls=%async_computation.29 | async-start | bytes 14417920 | tf_op jit(solution)/shard_map/reduce_scatter | solution.py:371
  1075.1 9.7 copy-start.15
  1075.1 9.7 copy-start.49
  1075.1 9.7 copy-start.59
  1075.1 11.0 copy-start.65
  1075.1 12.1 copy-start.6
  1075.1 12.1 copy-start.36
  1075.1 12.1 copy-start.47
  1075.2 328.6 %reduce-scatter.17.cloned.1.call-start = ((), (), s32[]{:S(2)}) async-start(), calls=%async_computation.25 | async-start | bytes 2949120 | tf_op jit(solution)/shard_map/reduce_scatter | solution.py:353
  1089.6 361.9 %reduce-scatter.19.cloned.1.call-start = ((), (), s32[]{:S(2)}) async-start(), calls=%async_computation.26 | async-start | bytes 5242880 | tf_op jit(solution)/shard_map/reduce_scatter | solution.py:359
  1101.9 423.8 %reduce-scatter.21.cloned.1.call-start = ((), (), s32[]{:S(2)}) async-start(), calls=%async_computation.27 | async-start | bytes 10485760 | tf_op jit(solution)/shard_map/reduce_scatter | solution.py:362
  1109.9 12.6 copy-start.38
  1109.9 12.6 copy-start.40
  1109.9 517.5 %reduce-scatter.15.cloned.1.call-start = ((), (), s32[]{:S(2)}) async-start(), calls=%async_computation.24 | async-start | bytes 15728640 | tf_op jit(solution)/shard_map/reduce_scatter | solution.py:350
  1131.9 540.9 %reduce-scatter.23.cloned.1.call-start = ((), (), s32[]{:S(2)}) async-start(), calls=%async_computation.28 | async-start | bytes 81920 | tf_op jit(solution)/shard_map/reduce_scatter | solution.py:368
  1132.8 1006.3 %all-reduce.15.cloned.1.call-start = ((), (), s32[]{:S(2)}) async-start(), calls=%async_computation.32 | async-start | bytes 31064064 | tf_op jit(solution)/shard_map/psum | solution.py:395
  1630.6 9.6 copy-start.83
  1663.6 51.8 %copy-start.63 = (f32[256]{0:T(256)S(1)}, f32[256]{0:T(256)}, u32[]{:S(2)}) copy-start(f32[256]{0:T(256)} %copy-done.62) | copy-start | bytes 3076
  (49 other events, 172.7 us)
Sparse Core Ops, SparseCore 0:
  9.6 26.7 all-gather.11
  41.6 30.4 all-gather.13
  73.7 32.8 all-gather.15
  108.0 82.0 all-gather.17
  191.6 58.2 all-gather.19
  251.3 127.6 all-gather.21
  380.5 123.3 all-gather.23
  505.5 83.3 all-gather.25
  1034.3 22.3 reduce-scatter.12
  1059.5 25.2 reduce-scatter.10
  1087.4 90.8 reduce-scatter.28
  1180.7 92.1 reduce-scatter.26
  1275.5 92.1 reduce-scatter.24
  1370.7 33.0 reduce-scatter.16
  1406.9 44.5 reduce-scatter.18
  1453.9 71.7 reduce-scatter.20
  1528.3 99.0 reduce-scatter.14
  1630.4 19.4 reduce-scatter.22
  1655.7 483.4 all-reduce.14
where the time goes:
time: 2180 us; the launch traced here: 2170 us
  waiting for transfers between devices  1300 us (60%)
  matrix products  285 us (13%)
  blocking collectives  283 us (13%)
  local copies, waits for them, and re-layouts  138 us (6%)
  other arithmetic  128 us (6%)
    psum x1, waiting for transfers between devices, per_device(): lax.psum(g_query.astype(jnp.bfloat16), ('replica', 'ctx'))  420 us
    all_to_all x1, blocking collectives, per_device(): lax.all_to_all(grad_payload, ('replica', 'fsdp', 'ctx'), split_axis=0, co...  121 us
    all_to_all x1, waiting for transfers between devices, per_device(): lax.all_to_all(payload, ('replica', 'fsdp', 'ctx'), split_axis=0, concat_...  112 us
    reduce_scatter x1, waiting for transfers between devices, per_device(): lax.psum_scatter(full_query.astype(jnp.bfloat16), 'fsdp', scatter_dimensi...  102 us
    all_to_all x1, waiting for transfers between devices, per_device(): lax.all_to_all(grad_rows, ('replica', 'fsdp', 'ctx'), split_axis=0, conca...  96 us
    reduce_scatter x1, waiting for transfers between devices, per_device(): lax.psum_scatter(full_share_gate.astype(jnp.bfloat16), 'fsdp', scatter_di...  94.8 us
    reduce_scatter x1, waiting for transfers between devices, per_device(): lax.psum_scatter(full_share_up.astype(jnp.bfloat16), 'fsdp', scatter_dime...  94.7 us
    dot_general x11, matrix products, matmul(): return jnp.dot(first_mat, second_mat, preferred_element_type=jnp.float32)  85.3 us
  transfers between devices with their start and end apart: 22, of which 18 were waited for; matrix products, arithmetic and copies ran while one was open for 16% of the time, Pallas kernels for 0%

commit v1 on v0

--- a/solution.py
+++ b/solution.py
@@ -43,6 +43,75 @@
 
 def silu_slope(gate_in, sigmoid_in):
     return sigmoid_in * (1.0 + gate_in * (1.0 - sigmoid_in))
+
+
+def masks(count):
+    found = []
+    mask = count // 2
+    while mask:
+        found.append(mask)
+        mask //= 2
+    return found
+
+
+def swap(values, axis, mask):
+    count = lax.axis_size(axis)
+    return lax.ppermute(values, axis, [(i, i ^ mask) for i in range(count)])
+
+
+def upper(axis, mask):
+    return (lax.axis_index(axis) // mask) % 2 == 1
+
+
+def halves(values, axis, mask, dim):
+    size = values.shape[dim] // 2
+    low = lax.slice_in_dim(values, 0, size, axis=dim)
+    high = lax.slice_in_dim(values, size, 2 * size, axis=dim)
+    up = upper(axis, mask)
+    return jnp.where(up, low, high), jnp.where(up, high, low)
+
+
+def join_halves(mine, other, axis, mask):
+    up = upper(axis, mask)
+    return jnp.concatenate([jnp.where(up, other, mine), jnp.where(up, mine, other)], axis=0)
+
+
+def gather_tokens(values):
+    for mask in masks(lax.axis_size("fsdp")):
+        values = jnp.concatenate([values, swap(values, "fsdp", mask)], axis=0)
+    return values
+
+
+def own_columns(values):
+    for mask in masks(lax.axis_size("fsdp")):
+        send, keep = halves(values, "fsdp", mask, 1)
+        values = jnp.concatenate([keep, swap(send, "fsdp", mask)], axis=0)
+    return values
+
+
+def scatter_rows(values, axis):
+    for mask in masks(lax.axis_size(axis)):
+        send, keep = halves(values, axis, mask, 0)
+        values = keep + swap(send.astype(jnp.bfloat16), axis, mask).astype(jnp.float32)
+    return values
+
+
+def sum_rows(values):
+    values = scatter_rows(values, "replica")
+    ctx_masks = masks(lax.axis_size("ctx"))[::-1]
+    for mask in ctx_masks:
+        send, keep = halves(values, "ctx", mask, 0)
+        values = keep + swap(send.astype(jnp.bfloat16), "ctx", mask).astype(jnp.float32)
+    values = values.astype(jnp.bfloat16)
+    for mask in ctx_masks[::-1]:
+        values = join_halves(values, swap(values, "ctx", mask), "ctx", mask)
+    for mask in masks(lax.axis_size("replica"))[::-1]:
+        values = join_halves(values, swap(values, "replica", mask), "replica", mask)
+    return values.astype(jnp.float32)
+
+
+def total(values):
+    return jnp.sum(lax.all_gather(values, ("replica", "fsdp", "ctx"), axis=0, tiled=True))
 
 
 def per_device(
@@ -84,6 +153,7 @@
         lax.all_gather(w_expand, "fsdp", axis=0, tiled=True),
         lax.all_gather(w_out, "fsdp", axis=0, tiled=True),
     )
+    valid_count = total(valid_mask).astype(jnp.float32)
     gain_one = gain_one.astype(jnp.float32)
     gain_latent = gain_latent.astype(jnp.float32)
     positions = (offset + jnp.arange(rows_dev)).astype(jnp.float32)
@@ -108,10 +178,10 @@
     rope_part = latent_raw[:, LATENT:]
     latent_own = rms_norm(latent_part, gain_latent).astype(jnp.bfloat16)
     rope_own = turn_key(rope_part).astype(jnp.bfloat16)
-    latent_all, rope_all = (
-        lax.all_gather(latent_own, "ctx", axis=0, tiled=True),
-        lax.all_gather(rope_own, "ctx", axis=0, tiled=True),
-    )
+    latent_rope = lax.all_gather(
+        jnp.concatenate([latent_own, rope_own], axis=1), "ctx", axis=0, tiled=True
+    )
+    latent_all, rope_all = latent_rope[:, :LATENT], latent_rope[:, LATENT:]
     key_count = latent_all.shape[0]
     expanded = (
         matmul(latent_all, expand_mat).astype(jnp.bfloat16).reshape(key_count, HEADS, NOPE + VDIM)
@@ -201,9 +271,11 @@
     picked = jnp.take(slot_out, slots, axis=0).reshape(rows_dev, top_count, D)
     final = mixed + share_out + jnp.sum(gates[:, :, None] * picked, axis=1)
     error_rows = final - target
-    valid_count, error_total = lax.psum(
-        (jnp.sum(valid_rows), jnp.sum(valid_rows[:, None] * error_rows * error_rows)),
-        ("replica", "fsdp", "ctx"),
+    error_total = total(
+        jnp.sum(
+            (valid_rows[:, None] * error_rows * error_rows).reshape(rows_dev, D // 128, 128),
+            axis=(0, 1),
+        )[None]
     )
     loss_value = error_total / (valid_count * D)
     grad_final = 2.0 / (valid_count * D) * valid_rows[:, None] * error_rows
@@ -257,14 +329,23 @@
         jnp.take(grad_slots, slots, axis=0).reshape(rows_dev, top_count, D), axis=1
     )
     grad_shared = grad_final.astype(jnp.bfloat16)
-    full_share_down = rows_dot(share_act, grad_shared)
+    g_share_down = sum_rows(
+        rows_dot(own_columns(share_act), gather_tokens(grad_shared))
+    )
     grad_share_act = cols_dot(grad_shared, share_down_mat)
     grad_share_gate = (grad_share_act * share_up_in * silu_slope(share_gate_in, share_sig)).astype(
         jnp.bfloat16
     )
     grad_share_up = (grad_share_act * share_gate_in * share_sig).astype(jnp.bfloat16)
-    full_share_gate = rows_dot(normed_two, grad_share_gate)
-    full_share_up = rows_dot(normed_two, grad_share_up)
+    normed_two_own = own_columns(normed_two)
+    share_width = grad_share_gate.shape[1]
+    g_share_both = sum_rows(
+        rows_dot(
+            normed_two_own,
+            gather_tokens(jnp.concatenate([grad_share_gate, grad_share_up], axis=1)),
+        )
+    )
+    g_share_gate, g_share_up = g_share_both[:, :share_width], g_share_both[:, share_width:]
     full_router = rows_dot(normed_two, grad_logits)
     grad_normed_two = (
         grad_normed_two
@@ -276,7 +357,7 @@
     grad_mixed_norm, gain_two_grad = norm_two_back(grad_normed_two)
     grad_mixed = grad_final + grad_mixed_norm
     grad_mix = grad_mixed.astype(jnp.bfloat16)
-    full_out = rows_dot(attended, grad_mix)
+    g_out = sum_rows(rows_dot(own_columns(attended), gather_tokens(grad_mix)))
     grad_att = cols_dot(grad_mix, out_mat).astype(jnp.bfloat16).reshape(rows_dev, HEADS, VDIM)
     scores = score_rows()
     prob_rows = jnp.exp(scores - log_total)
@@ -303,14 +384,13 @@
     full_expand = rows_dot(latent_all, grad_expanded)
     grad_latent_all = cols_dot(grad_expanded, expand_mat)
     grad_rope_all = jnp.sum(grad_key[..., NOPE:], axis=1)
-    grad_latent_own, grad_rope_own = (
-        lax.psum_scatter(
-            grad_latent_all.astype(jnp.bfloat16), "ctx", scatter_dimension=0, tiled=True
-        ).astype(jnp.float32),
-        lax.psum_scatter(
-            grad_rope_all.astype(jnp.bfloat16), "ctx", scatter_dimension=0, tiled=True
-        ).astype(jnp.float32),
-    )
+    grad_latent_rope = lax.psum_scatter(
+        jnp.concatenate([grad_latent_all, grad_rope_all], axis=1).astype(jnp.bfloat16),
+        "ctx",
+        scatter_dimension=0,
+        tiled=True,
+    ).astype(jnp.float32)
+    grad_latent_own, grad_rope_own = grad_latent_rope[:, :LATENT], grad_latent_rope[:, LATENT:]
     _, latent_back = jax.vjp(rms_norm, latent_part, gain_latent)
     grad_latent_part, gain_latent_grad = latent_back(grad_latent_own)
     _, rope_back = jax.vjp(turn_key, rope_part)
@@ -325,84 +405,52 @@
         .astype(jnp.bfloat16)
         .reshape(rows_dev, HEADS * (NOPE + ROPE))
     )
-    full_query = rows_dot(normed, grad_query_raw)
-    full_latent = rows_dot(normed, grad_latent_raw)
+    query_width = grad_query_raw.shape[1]
+    own_first = rows_dot(
+        own_columns(normed),
+        gather_tokens(jnp.concatenate([grad_query_raw, grad_latent_raw], axis=1)),
+    )
     grad_normed = cols_dot(grad_query_raw, query_mat) + cols_dot(grad_latent_raw, latent_mat)
     _, norm_one_back = jax.vjp(rms_norm, resid, gain_one)
     grad_resid_norm, gain_one_grad = norm_one_back(grad_normed)
     input_grad = grad_mixed + grad_resid_norm
-    (
-        g_gain_one,
-        g_query,
-        g_latent,
-        g_gain_latent,
-        g_expand,
-        g_out,
-        g_gain_two,
-        g_router,
-        g_share_gate,
-        g_share_up,
-        g_share_down,
-    ) = (
-        lax.psum_scatter(
-            gain_one_grad.astype(jnp.bfloat16), "fsdp", scatter_dimension=0, tiled=True
-        ).astype(jnp.float32),
-        lax.psum_scatter(
-            full_query.astype(jnp.bfloat16), "fsdp", scatter_dimension=0, tiled=True
-        ).astype(jnp.float32),
-        lax.psum_scatter(
-            full_latent.astype(jnp.bfloat16), "fsdp", scatter_dimension=0, tiled=True
-        ).astype(jnp.float32),
-        lax.psum_scatter(
-            gain_latent_grad.astype(jnp.bfloat16), "fsdp", scatter_dimension=0, tiled=True
-        ).astype(jnp.float32),
-        lax.psum_scatter(
-            full_expand.astype(jnp.bfloat16), "fsdp", scatter_dimension=0, tiled=True
-        ).astype(jnp.float32),
-        lax.psum_scatter(
-            full_out.astype(jnp.bfloat16), "fsdp", scatter_dimension=0, tiled=True
-        ).astype(jnp.float32),
-        lax.psum_scatter(
-            gain_two_grad.astype(jnp.bfloat16), "fsdp", scatter_dimension=0, tiled=True
-        ).astype(jnp.float32),
-        lax.psum_scatter(
-            full_router.astype(jnp.bfloat16), "fsdp", scatter_dimension=0, tiled=True
-        ).astype(jnp.float32),
-        lax.psum_scatter(
-            full_share_gate.astype(jnp.bfloat16), "fsdp", scatter_dimension=0, tiled=True
-        ).astype(jnp.float32),
-        lax.psum_scatter(
-            full_share_up.astype(jnp.bfloat16), "fsdp", scatter_dimension=0, tiled=True
-        ).astype(jnp.float32),
-        lax.psum_scatter(
-            full_share_down.astype(jnp.bfloat16), "fsdp", scatter_dimension=0, tiled=True
-        ).astype(jnp.float32),
-    )
-    (
-        g_gain_one,
-        g_query,
-        g_latent,
-        g_gain_latent,
-        g_expand,
-        g_out,
-        g_gain_two,
-        g_router,
-        g_share_gate,
-        g_share_up,
-        g_share_down,
-    ) = (
-        lax.psum(g_gain_one.astype(jnp.bfloat16), ("replica", "ctx")).astype(jnp.float32),
-        lax.psum(g_query.astype(jnp.bfloat16), ("replica", "ctx")).astype(jnp.float32),
-        lax.psum(g_latent.astype(jnp.bfloat16), ("replica", "ctx")).astype(jnp.float32),
-        lax.psum(g_gain_latent.astype(jnp.bfloat16), ("replica", "ctx")).astype(jnp.float32),
-        lax.psum(g_expand.astype(jnp.bfloat16), ("replica", "ctx")).astype(jnp.float32),
-        lax.psum(g_out.astype(jnp.bfloat16), ("replica", "ctx")).astype(jnp.float32),
-        lax.psum(g_gain_two.astype(jnp.bfloat16), ("replica", "ctx")).astype(jnp.float32),
-        lax.psum(g_router.astype(jnp.bfloat16), ("replica", "ctx")).astype(jnp.float32),
-        lax.psum(g_share_gate.astype(jnp.bfloat16), ("replica", "ctx")).astype(jnp.float32),
-        lax.psum(g_share_up.astype(jnp.bfloat16), ("replica", "ctx")).astype(jnp.float32),
-        lax.psum(g_share_down.astype(jnp.bfloat16), ("replica", "ctx")).astype(jnp.float32),
-    )
+    fsdp_count = lax.axis_size("fsdp")
+    own_expand = scatter_rows(full_expand, "fsdp")
+    own_expand_rows = own_expand.shape[0]
+    pieces = own_first.shape[0] // own_expand_rows
+    expand_width = own_expand.shape[1] // pieces
+    own_expand = jnp.concatenate(
+        [own_expand[:, i * expand_width : (i + 1) * expand_width] for i in range(pieces)], axis=0
+    )
+    latent_column = jnp.concatenate(
+        [
+            gain_latent_grad.reshape(fsdp_count, own_expand_rows),
+            jnp.zeros((fsdp_count, (D - LATENT) // fsdp_count), jnp.float32),
+        ],
+        axis=1,
+    ).reshape(D, 1)
+    small = scatter_rows(
+        jnp.concatenate(
+            [full_router, gain_one_grad[:, None], gain_two_grad[:, None], latent_column], axis=1
+        ),
+        "fsdp",
+    )
+    last = sum_rows(jnp.concatenate([own_first, own_expand, small], axis=1))
+    g_query, g_latent = last[:, :query_width], last[:, query_width : own_first.shape[1]]
+    start = own_first.shape[1]
+    g_expand = jnp.concatenate(
+        [
+            last[i * own_expand_rows : (i + 1) * own_expand_rows, start : start + expand_width]
+            for i in range(pieces)
+        ],
+        axis=1,
+    )
+    start += expand_width
+    g_router = last[:, start : start + expert_count]
+    start += expert_count
+    g_gain_one = last[:, start]
+    g_gain_two = last[:, start + 1]
+    g_gain_latent = last[:own_expand_rows, start + 2]
     return (
         final.astype(jnp.bfloat16).reshape(1, rows_dev, D),
         loss_value,

time: 2180 us -> 1900 us (0.87)
  waiting for transfers between devices: 1300 us -> 799 us
  other arithmetic: 128 us -> 242 us
  local copies, waits for them, and re-layouts: 138 us -> 208 us
  starting transfers between devices: 18.6 us -> 57 us
    ppermute x0 -> x44, waiting for transfers between devices: none -> 559 us  [swap(): return lax.ppermute(values, axis, [(i, i ^ mask) for i in range(count)])]
    reduce_scatter x10 -> x1, waiting for transfers between devices: 503 us -> 0.01 us  [per_device(): lax.psum_scatter(jnp.concatenate([grad_latent_all, grad_rope_all], axis=1...]
    psum x1 -> x0, waiting for transfers between devices: 420 us -> none  [per_device(): lax.psum(g_query.astype(jnp.bfloat16), ('replica', 'ctx'))]
    all_gather x1 -> x2, blocking collectives: 13.4 us -> 250 us  [total(): lax.all_gather(values, ('replica', 'fsdp', 'ctx'), axis=0, tiled=True)]
    all_to_all x1 -> x0, blocking collectives: 121 us -> none  [per_device(): lax.all_to_all(grad_payload, ('replica', 'fsdp', 'ctx'), split_axis=0, co...]
    all_to_all x1, waiting for transfers between devices: 96 us -> 0.01 us  [per_device(): lax.all_to_all(grad_rows, ('replica', 'fsdp', 'ctx'), split_axis=0, conca...]
    psum x2 -> x0, blocking collectives: 80.8 us -> none  [the longest x1 40.5 us: per_device(): lax.psum((jnp.sum(valid_rows), jnp.sum(valid_rows[:, None] * error_rows *...]
    concatenate x1 -> x20, other arithmetic: 0.01 us -> 42.3 us  [the longest x4 22.1 us: gather_tokens(): values = jnp.concatenate([values, swap(values, 'fsdp', mask)], axis=0)]
  transfers between devices with their start and end apart: 22 -> 57, of which waited for: 18 -> 26; matrix products, arithmetic and copies ran while one was open for 16% -> 36% of each run, Pallas kernels for 0% -> 0%
where the time goes in v1:
time: 1900 us; the launch traced here: 1890 us
  waiting for transfers between devices  799 us (42%)
  matrix products  291 us (15%)
  blocking collectives  273 us (14%)
  other arithmetic  242 us (13%)
  local copies, waits for them, and re-layouts  208 us (11%)
  starting transfers between devices  57 us (3%)
  between operations  19 us (1%)
    ppermute x44, waiting for transfers between devices, swap(): return lax.ppermute(values, axis, [(i, i ^ mask) for i in range(count)])  559 us
    all_gather x2, blocking collectives, total(): lax.all_gather(values, ('replica', 'fsdp', 'ctx'), axis=0, tiled=True)  250 us
    all_to_all x1, waiting for transfers between devices, per_device(): lax.all_to_all(payload, ('replica', 'fsdp', 'ctx'), split_axis=0, concat_...  112 us
    dot_general x11, matrix products, matmul(): return jnp.dot(first_mat, second_mat, preferred_element_type=jnp.float32)  86.3 us
    dot_general x9, matrix products, rows_dot(): lax.dot_general(first_mat, second_mat, (((0,), (0,)), ((), ())), preferre...  79.4 us
    dot_general x11, matrix products, cols_dot(): lax.dot_general(first_mat, second_mat, (((1,), (1,)), ((), ())), preferre...  68.1 us
    all_gather x1, waiting for transfers between devices, per_device(): lax.all_gather(w_query, 'fsdp', axis=0, tiled=True)  55.6 us
  transfers between devices with their start and end apart: 57, of which 26 were waited for; matrix products, arithmetic and copies ran while one was open for 36% of the time, Pallas kernels for 0%

profile of v1, /device:TPU:0, one launch (start us, length us, event | category | flops | bytes accessed | tf_op | source)
XLA Modules:
  0.0 1890.2 jit_solution(16215891558600233207)
XLA Ops:
  24.5 11.9 all-gather.15.cloned.1.call-done
  55.2 17.9 all-gather.17.cloned.1.call-done
  73.1 34.4 %all-gather.19.cloned.1.call-done = bf16[512,4096]{1,0:T(8,128)(2,1)} async-done(((bf16[128,4096]{1,0:T(8,128)(2,1)}), bf16[512,4096]{1,0:T(8,128)(2,1)}) %all-gather.19.cloned.1.call-update) | async-done | bytes 4194320 | tf_op jit(solution)/shard_map/all_gather | solution.py:153
  107.5 11.3 convolution_convert_fusion.1
  118.8 11.7 copy.202
  135.5 55.6 %all-gather.21.cloned.1.call-done = bf16[2048,3072]{1,0:T(8,128)(2,1)} async-done(((bf16[512,3072]{1,0:T(8,128)(2,1)}), bf16[2048,3072]{1,0:T(8,128)(2,1)}) %all-gather.21.cloned.1.call-update) | async-done | bytes 12582928 | tf_op jit(solution)/shard_map/all_gather | solution.py:150
  191.0 16.7 copy.168
  207.8 7.0 fusion.75
  217.6 10.5 fusion
  228.1 8.2 exponential_reduce_fusion
  237.0 8.9 fusion.70
  260.7 8.7 gather_fusion
  280.0 111.6 %all-to-all-done = bf16[32,40,2048]{2,1,0:T(8,128)(2,1)} async-done(((bf16[32,40,2048]{2,1,0:T(8,128)(2,1)}), bf16[32,40,2048]{2,1,0:T(8,128)(2,1)}, u32[]{:S(2)}, u32[]{:S(2)}) %all-to-all-start) | async-done | bytes 5242912 | tf_op jit(solution)/shard_map/all_to_all | solution.py:253
  391.6 9.0 fusion.47
  400.6 9.7 multiply_convert_fusion.3
  416.3 7.6 all-to-all-start.1
  423.9 173.3 %all-gather.5 = s32[32,1,256]{2,1,0:T(1,128)S(1)} all-gather(s32[1,1,256]{2,1,0:T(1,128)S(1)} %bitcast.228), channel_id=1, replica_groups=mesh['replica'=2,'fsdp'=4,'ctx'=4] {'replica','fsdp','ctx'}, dimensions={0}, use_global_device_ids=true | all-gather | bytes 33792 | tf_op jit(solution)/shard_map/all_gather | solution.py:114
  607.4 9.3 fusion.155
  616.7 10.6 multiply_convert_fusion.6
  634.0 7.9 gather_fusion.2
  652.4 10.1 multiply_reduce_fusion.2
  662.5 12.5 fusion.148
  683.1 33.6 %collective-permute-done.34 = bf16[256,1408]{1,0:T(8,128)(2,1)} collective-permute-done((bf16[256,1408]{1,0:T(8,128)(2,1)}, bf16[256,1408]{1,0:T(8,128)(2,1)}, u32[]{:S(2)}, u32[]{:S(2)}) %collective-permute-start.34) | collective-permute-done | bytes 720928 | tf_op jit(solution)/shard_map/ppermute | solution.py:59
  726.4 9.6 multiply_convert_fusion.4
  766.7 8.8 gather_fusion.1
  784.4 45.9 %collective-permute-done.26 = bf16[256,5632]{1,0:T(8,128)(2,1)} collective-permute-done((bf16[256,5632]{1,0:T(8,128)(2,1)}, bf16[256,5632]{1,0:T(8,128)(2,1)}, u32[]{:S(2)}, u32[]{:S(2)}) %collective-permute-start.26) | collective-permute-done | bytes 2883616 | tf_op jit(solution)/shard_map/ppermute | solution.py:59
  852.3 35.9 %collective-permute-done.39 = bf16[176,2048]{1,0:T(8,128)(2,1)} collective-permute-done((bf16[176,2048]{1,0:T(8,128)(2,1)}, bf16[176,2048]{1,0:T(8,128)(2,1)}, u32[]{:S(2)}, u32[]{:S(2)}) %collective-permute-start.39) | collective-permute-done | bytes 720928 | tf_op jit(solution)/shard_map/ppermute | solution.py:59
  899.8 16.4 collective-permute-done.40
  917.0 18.0 collective-permute-done.41
  936.9 77.0 %all-gather.4 = f32[32,1,128]{2,1,0:T(1,128)S(1)} all-gather(f32[1,1,128]{2,1,0:T(1,128)S(1)} %bitcast.233), channel_id=2, replica_groups=mesh['replica'=2,'fsdp'=4,'ctx'=4] {'replica','fsdp','ctx'}, dimensions={0}, use_global_device_ids=true | all-gather | bytes 16896 | tf_op jit(solution)/shard_map/all_gather | solution.py:114
  1021.8 20.0 %fusion.1 = f32[512,5632]{1,0:T(8,128)} fusion(bf16[512,5632]{1,0:T(8,128)(2,1)} %collective-permute-done.27, bf16[256,5632]{1,0:T(8,128)(2,1)} %collective-permute-done.26, bf16[256,2816]{1,0:T(8,128)(2,1)S(1)} %copy-done.36, bf16[256,2816]{1,0:T(8,128)(2,1)S(1)} %copy-done.39, bf16[512,512]{1,0:T(8,128)(2,1)} %collective-permute-done.25, ...), kind=kOutput, calls=%fused_computation.13 | convolution fusion | flops 5953814528 | bytes 24117248 | tf_op jit(solution)/shard_map/dot_general | solution.py:29
  1049.7 9.0 multiply_convert_fusion.1
  1073.2 71.0 %collective-permute-done.28 = bf16[256,5632]{1,0:T(8,128)(2,1)} collective-permute-done((bf16[256,5632]{1,0:T(8,128)(2,1)}, bf16[256,5632]{1,0:T(8,128)(2,1)}, u32[]{:S(2)}, u32[]{:S(2)}) %collective-permute-start.28) | collective-permute-done | bytes 2883616 | tf_op jit(solution)/shard_map/ppermute | solution.py:59
  1157.3 8.6 convolution_bitcast_fusion.2
  1165.9 30.9 %collective-permute-done.29 = bf16[128,5632]{1,0:T(8,128)(2,1)S(1)} collective-permute-done((bf16[128,5632]{1,0:T(8,128)(2,1)S(1)}, bf16[128,5632]{1,0:T(8,128)(2,1)S(1)}, u32[]{:S(2)}, u32[]{:S(2)}) %collective-permute-start.29) | collective-permute-done | bytes 1441824 | tf_op jit(solution)/shard_map/ppermute | solution.py:59
  1197.5 8.2 convolution_bitcast_fusion
  1205.7 22.8 %collective-permute-done.30 = bf16[64,5632]{1,0:T(8,128)(2,1)S(1)} collective-permute-done((bf16[64,5632]{1,0:T(8,128)(2,1)S(1)}, bf16[64,5632]{1,0:T(8,128)(2,1)S(1)}, u32[]{:S(2)}, u32[]{:S(2)}) %collective-permute-start.30) | collective-permute-done | bytes 720928 | tf_op jit(solution)/shard_map/ppermute | solution.py:59
  1228.8 8.2 convolution_bitcast_fusion.1
  1237.1 23.7 %collective-permute-done.31 = bf16[64,5632]{1,0:T(8,128)(2,1)S(1)} collective-permute-done((bf16[64,5632]{1,0:T(8,128)(2,1)S(1)}, bf16[64,5632]{1,0:T(8,128)(2,1)S(1)}, u32[]{:S(2)}, u32[]{:S(2)}) %collective-permute-start.31) | collective-permute-done | bytes 720928 | tf_op jit(solution)/shard_map/ppermute | solution.py:59
  1268.9 7.9 gather_fusion.3
  1287.3 8.6 reduce_sum.288
  1295.9 8.1 convolution_add_fusion.3
  1320.2 9.6 convert_bitcast_fusion
  1329.8 14.3 multiply_reduce_fusion
  1344.2 15.6 multiply_convert_fusion
  1373.6 8.2 pad_maximum_fusion
  1381.8 9.1 convolution_convert_fusion.3
  1392.6 7.0 fusion.88
  1405.2 9.3 multiply_bitcast_fusion.1
  1417.9 8.0 fusion.157
  1440.8 24.4 %collective-permute-done.4 = bf16[256,4096]{1,0:T(8,128)(2,1)} collective-permute-done((bf16[256,4096]{1,0:T(8,128)(2,1)}, bf16[256,4096]{1,0:T(8,128)(2,1)}, u32[]{:S(2)}, u32[]{:S(2)}) %collective-permute-start.4) | collective-permute-done | bytes 2097184 | tf_op jit(solution)/shard_map/ppermute | solution.py:59
  1470.4 39.1 %collective-permute-done.6 = bf16[1024,19]{1,0:T(8,128)(2,1)S(1)} collective-permute-done((bf16[1024,19]{1,0:T(8,128)(2,1)S(1)}, bf16[1024,19]{1,0:T(8,128)(2,1)S(1)}, u32[]{:S(2)}, u32[]{:S(2)}) %collective-permute-start.6) | collective-permute-done | bytes 38944 | tf_op jit(solution)/shard_map/ppermute | solution.py:59
  1509.5 10.1 pad_maximum_fusion.5
  1537.2 15.2 fusion.10
  1552.4 11.7 concatenate.162
  1583.8 44.9 %collective-permute-done.8 = bf16[256,4691]{0,1:T(8,128)(2,1)} collective-permute-done((bf16[256,4691]{0,1:T(8,128)(2,1)}, bf16[256,4691]{0,1:T(8,128)(2,1)}, u32[]{:S(2)}, u32[]{:S(2)}) %collective-permute-start.8) | collective-permute-done | bytes 2401824 | tf_op jit(solution)/shard_map/ppermute | solution.py:59
  1653.5 24.0 %collective-permute-done.9 = bf16[128,4691]{0,1:T(8,128)(2,1)} collective-permute-done((bf16[128,4691]{0,1:T(8,128)(2,1)}, bf16[128,4691]{0,1:T(8,128)(2,1)}, u32[]{:S(2)}, u32[]{:S(2)}) %collective-permute-start.9) | collective-permute-done | bytes 1200928 | tf_op jit(solution)/shard_map/ppermute | solution.py:59
  1683.7 28.5 %collective-permute-done.33 = bf16[256,5632]{1,0:T(8,128)(2,1)} collective-permute-done((bf16[256,5632]{1,0:T(8,128)(2,1)}, bf16[256,5632]{1,0:T(8,128)(2,1)}, u32[]{:S(2)}, u32[]{:S(2)}) %collective-permute-start.33) | collective-permute-done | bytes 2883616 | tf_op jit(solution)/shard_map/ppermute | solution.py:59
  1719.9 22.8 %collective-permute-done.21 = bf16[64,2048]{1,0:T(8,128)(2,1)S(1)} collective-permute-done((bf16[64,2048]{1,0:T(8,128)(2,1)S(1)}, bf16[64,2048]{1,0:T(8,128)(2,1)S(1)}, u32[]{:S(2)}, u32[]{:S(2)}) %collective-permute-start.21) | collective-permute-done | bytes 262176 | tf_op jit(solution)/shard_map/ppermute | solution.py:59
  1743.8 11.6 collective-permute-done.11
  1757.4 8.5 maximum_convert_fusion
  1770.7 21.6 %collective-permute-done.12 = bf16[128,4691]{0,1:T(8,128)(2,1)} collective-permute-done((bf16[128,4691]{0,1:T(8,128)(2,1)}, bf16[128,4691]{0,1:T(8,128)(2,1)}, u32[]{:S(2)}, u32[]{:S(2)}) %collective-permute-start.12) | collective-permute-done | bytes 1200928 | tf_op jit(solution)/shard_map/ppermute | solution.py:59
  1805.0 9.5 fusion.150
  1820.7 37.1 %collective-permute-done.13 = bf16[256,4691]{0,1:T(8,128)(2,1)} collective-permute-done((bf16[256,4691]{0,1:T(8,128)(2,1)}, bf16[256,4691]{0,1:T(8,128)(2,1)}, u32[]{:S(2)}, u32[]{:S(2)}) %collective-permute-start.13) | collective-permute-done | bytes 2401824 | tf_op jit(solution)/shard_map/ppermute | solution.py:59
  (578 shorter events, 444.4 us)
Async XLA Ops:
  7.2 403.1 %copy-start = (bf16[1,704,2048]{2,1,0:T(8,128)(2,1)S(1)}, bf16[1,704,2048]{2,1,0:T(8,128)(2,1)}, u32[]{:S(2)}) copy-start(bf16[1,704,2048]{2,1,0:T(8,128)(2,1)} %param.39) | copy-start | bytes 8650756
  7.2 29.2 %all-gather.15.cloned.1.call-start = ((), (), s32[]{:S(2)}) async-start(), calls=%async_computation.5 | async-start | bytes 2949120 | tf_op jit(solution)/shard_map/all_gather | solution.py:151
  7.9 65.1 %all-gather.17.cloned.1.call-start = ((), (), s32[]{:S(2)}) async-start(), calls=%async_computation.6 | async-start | bytes 1474560 | tf_op jit(solution)/shard_map/all_gather | solution.py:181
  14.9 192.9 %copy-start.75 = (f32[4,1,512]{2,1,0:T(1,128)}, f32[4,1,512]{2,1,0:T(1,128)S(1)}, u32[]{:S(2)}) copy-start(f32[4,1,512]{2,1,0:T(1,128)S(1)} %convert_element_type.357) | copy-start | bytes 24580
  21.9 185.8 %copy-start.81 = (f32[256]{0:T(256)}, f32[256]{0:T(256)S(1)}, u32[]{:S(2)}) copy-start(f32[256]{0:T(256)S(1)} %fusion.131) | copy-start | bytes 3076
  40.4 174.6 %copy-start.71 = (f32[256,32]{0,1:T(8,128)}, f32[256,32]{0,1:T(8,128)S(1)}, u32[]{:S(2)}) copy-start(f32[256,32]{0,1:T(8,128)S(1)} %get-tuple-element.219) | copy-start | bytes 98308
  41.1 66.3 %all-gather.19.cloned.1.call-start = ((), (), s32[]{:S(2)}) async-start(), calls=%async_computation.7 | async-start | bytes 5242880 | tf_op jit(solution)/shard_map/all_gather | solution.py:153
  41.9 149.2 %all-gather.21.cloned.1.call-start = ((), (), s32[]{:S(2)}) async-start(), calls=%async_computation.8 | async-start | bytes 15728640 | tf_op jit(solution)/shard_map/all_gather | solution.py:150
  42.5 208.3 %all-gather.23.cloned.1.call-start = ((), (), s32[]{:S(2)}) async-start(), calls=%async_computation.9 | async-start | bytes 10485760 | tf_op jit(solution)/shard_map/all_gather | solution.py:154
  43.1 564.3 %all-gather.25.cloned.1.call-start = ((), (), s32[]{:S(2)}) async-start(), calls=%async_computation.10 | async-start | bytes 14417920 | tf_op jit(solution)/shard_map/all_gather | solution.py:217
  43.7 573.1 %all-gather.27.cloned.1.call-start = ((), (), s32[]{:S(2)}) async-start(), calls=%async_computation.11 | async-start | bytes 14417920 | tf_op jit(solution)/shard_map/all_gather | solution.py:218
  51.4 205.7 %copy-start.79 = (f32[4,1,512]{2,1,0:T(1,128)}, f32[4,1,512]{2,1,0:T(1,128)S(1)}, u32[]{:S(2)}) copy-start(f32[4,1,512]{2,1,0:T(1,128)S(1)} %convert_element_type.359) | copy-start | bytes 24580
  55.2 181.1 %copy-start.46 = (pred[256,1024]{1,0:T(8,128)(4,1)}, pred[256,1024]{1,0:T(8,128)(4,1)S(1)}, u32[]{:S(2)}) copy-start(pred[256,1024]{1,0:T(8,128)(4,1)S(1)} %broadcast_compare_fusion) | copy-start | bytes 786436
  274.5 117.0 %all-to-all-start = ((bf16[32,40,2048]{2,1,0:T(8,128)(2,1)}), bf16[32,40,2048]{2,1,0:T(8,128)(2,1)}, u32[]{:S(2)}, u32[]{:S(2)}) async-start(bf16[32,40,2048]{2,1,0:T(8,128)(2,1)} %bitcast.192), calls=%async_computation | async-start | bytes 10485760 | tf_op jit(solution)/shard_map/all_to_all | solution.py:253
  279.2 383.3 %all-gather.29.cloned.1.call-start = ((), (), s32[]{:S(2)}) async-start(), calls=%async_computation.12 | async-start | bytes 14417920 | tf_op jit(solution)/shard_map/all_gather | solution.py:219
  416.3 182.4 %copy-start.91 = (bf16[512,16]{0,1:T(8,128)(2,1)S(1)}, bf16[512,16]{0,1:T(8,128)(2,1)}, u32[]{:S(2)}) copy-start(bf16[512,16]{0,1:T(8,128)(2,1)} %param.33) | copy-start | bytes 49156
  416.3 211.1 %all-to-all-start.1 = ((bf16[32,40,2048]{2,1,0:T(8,128)(2,1)}), bf16[32,40,2048]{2,1,0:T(8,128)(2,1)}, u32[]{:S(2)}, u32[]{:S(2)}) async-start(bf16[32,40,2048]{2,1,0:T(8,128)(2,1)} %bitcast.205), calls=%async_computation.1 | async-start | bytes 10485760 | tf_op jit(solution)/shard_map/all_to_all | solution.py:264
  675.0 47.8 %collective-permute-start.36 = (bf16[256,2048]{1,0:T(8,128)(2,1)}, bf16[256,2048]{1,0:T(8,128)(2,1)}, u32[]{:S(2)}, u32[]{:S(2)}) collective-permute-start(bf16[256,2048]{1,0:T(8,128)(2,1)} %get-tuple-element.147), channel_id=1, source_target_pairs={{0,8},{4,12},{8,0},{12,4},{1,9},{5,13},{9,1},{13,5},{2,10},{6,14},... | collective-permute-start | bytes 3145736 | tf_op jit(solution)/shard_map/ppermute | solution.py:59
  676.3 40.5 %collective-permute-start.34 = (bf16[256,1408]{1,0:T(8,128)(2,1)}, bf16[256,1408]{1,0:T(8,128)(2,1)}, u32[]{:S(2)}, u32[]{:S(2)}) collective-permute-start(bf16[256,1408]{1,0:T(8,128)(2,1)} %get-tuple-element.188), channel_id=1, source_target_pairs={{0,8},{4,12},{8,0},{12,4},{1,9},{5,13},{9,1},{13,5},{2,10},{6,14},... | collective-permute-start | bytes 2162696 | tf_op jit(solution)/shard_map/ppermute | solution.py:59
  679.1 214.1 %collective-permute-start = (bf16[256,1024]{1,0:T(8,128)(2,1)}, bf16[256,1024]{1,0:T(8,128)(2,1)}, u32[]{:S(2)}, u32[]{:S(2)}) collective-permute-start(bf16[256,1024]{1,0:T(8,128)(2,1)} %get-tuple-element.208), channel_id=1, source_target_pairs={{0,8},{4,12},{8,0},{12,4},{1,9},{5,13},{9,1},{13,5},{2,10},{6,14},... | collective-permute-start | bytes 1572872 | tf_op jit(solution)/shard_map/ppermute | solution.py:59
  722.8 17.1 collective-permute-start.35
  726.1 28.5 %collective-permute-start.37 = (bf16[512,2048]{1,0:T(8,128)(2,1)}, bf16[512,2048]{1,0:T(8,128)(2,1)}, u32[]{:S(2)}, u32[]{:S(2)}) collective-permute-start(bf16[512,2048]{1,0:T(8,128)(2,1)} %pad_maximum_fusion.12), channel_id=1, source_target_pairs={{0,4},{4,0},{8,12},{12,8},{1,5},{5,1},{9,13},{13,9},{2,6},{6,2},{1... | collective-permute-start | bytes 6291464 | tf_op jit(solution)/shard_map/ppermute | solution.py:59
  738.5 91.8 %collective-permute-start.26 = (bf16[256,5632]{1,0:T(8,128)(2,1)}, bf16[256,5632]{1,0:T(8,128)(2,1)}, u32[]{:S(2)}, u32[]{:S(2)}) collective-permute-start(bf16[256,5632]{1,0:T(8,128)(2,1)} %pad_maximum_fusion.6), channel_id=1, source_target_pairs={{0,8},{4,12},{8,0},{12,4},{1,9},{5,13},{9,1},{13,5},{2,10},{6,14},... | collective-permute-start | bytes 8650760 | tf_op jit(solution)/shard_map/ppermute | solution.py:59
  761.5 74.4 %collective-permute-start.38 = (bf16[352,2048]{1,0:T(8,128)(2,1)}, bf16[352,2048]{1,0:T(8,128)(2,1)}, u32[]{:S(2)}, u32[]{:S(2)}) collective-permute-start(bf16[352,2048]{1,0:T(8,128)(2,1)} %select_convert_fusion.4), channel_id=1, source_target_pairs={{0,16},{16,0},{1,17},{17,1},{2,18},{18,2},{3,19},{19,3},{4,20},{20... | collective-permute-start | bytes 4325384 | tf_op jit(solution)/shard_map/ppermute | solution.py:59
  780.8 268.9 %all-to-all-start.2 = ((bf16[32,40,2048]{2,1,0:T(8,128)(2,1)}), bf16[32,40,2048]{2,1,0:T(8,128)(2,1)}, u32[]{:S(2)}, u32[]{:S(2)}) async-start(bf16[32,40,2048]{2,1,0:T(8,128)(2,1)} %bitcast.191), calls=%async_computation.2 | async-start | bytes 10485760 | tf_op jit(solution)/shard_map/all_to_all | solution.py:299
  835.9 186.0 %collective-permute-start.27 = (bf16[512,5632]{1,0:T(8,128)(2,1)}, bf16[512,5632]{1,0:T(8,128)(2,1)}, u32[]{:S(2)}, u32[]{:S(2)}) collective-permute-start(bf16[512,5632]{1,0:T(8,128)(2,1)} %pad_maximum_fusion.2), channel_id=1, source_target_pairs={{0,4},{4,0},{8,12},{12,8},{1,5},{5,1},{9,13},{13,9},{2,6},{6,2},{1... | collective-permute-start | bytes 17301512 | tf_op jit(solution)/shard_map/ppermute | solution.py:59
  840.7 47.5 %collective-permute-start.39 = (bf16[176,2048]{1,0:T(8,128)(2,1)}, bf16[176,2048]{1,0:T(8,128)(2,1)}, u32[]{:S(2)}, u32[]{:S(2)}) collective-permute-start(bf16[176,2048]{1,0:T(8,128)(2,1)} %select_convert_fusion.9), channel_id=1, source_target_pairs={{0,1},{1,0},{2,3},{3,2},{4,5},{5,4},{6,7},{7,6},{8,9},{9,8},{10,11... | collective-permute-start | bytes 2162696 | tf_op jit(solution)/shard_map/ppermute | solution.py:59
  842.7 53.0 %collective-permute-start.24 = (bf16[256,1024]{1,0:T(8,128)(2,1)}, bf16[256,1024]{1,0:T(8,128)(2,1)}, u32[]{:S(2)}, u32[]{:S(2)}) collective-permute-start(bf16[256,1024]{1,0:T(8,128)(2,1)} %get-tuple-element.196), channel_id=1, source_target_pairs={{0,8},{4,12},{8,0},{12,4},{1,9},{5,13},{9,1},{13,5},{2,10},{6,14},... | collective-permute-start | bytes 1572872 | tf_op jit(solution)/shard_map/ppermute | solution.py:59
  852.2 46.5 %collective-permute-start.14 = (bf16[256,1024]{1,0:T(8,128)(2,1)S(1)}, bf16[256,1024]{1,0:T(8,128)(2,1)S(1)}, u32[]{:S(2)}, u32[]{:S(2)}) collective-permute-start(bf16[256,1024]{1,0:T(8,128)(2,1)S(1)} %get-tuple-element.202), channel_id=1, source_target_pairs={{0,8},{4,12},{8,0},{12,4},{1,9},{5,13},{9,1},{13,5},{2,10},{6,14},... | collective-permute-start | bytes 1572872 | tf_op jit(solution)/shard_map/ppermute | solution.py:59
  890.5 25.7 %collective-permute-start.40 = (bf16[88,2048]{1,0:T(8,128)(2,1)S(1)}, bf16[88,2048]{1,0:T(8,128)(2,1)S(1)}, u32[]{:S(2)}, u32[]{:S(2)}) collective-permute-start(bf16[88,2048]{1,0:T(8,128)(2,1)S(1)} %select_convert_fusion.13), channel_id=1, source_target_pairs={{0,2},{1,3},{2,0},{3,1},{4,6},{5,7},{6,4},{7,5},{8,10},{9,11},{10,... | collective-permute-start | bytes 1081352 | tf_op jit(solution)/shard_map/ppermute | solution.py:59
  895.7 641.5 %collective-permute-start.1 = (bf16[512,512]{1,0:T(8,128)(2,1)}, bf16[512,512]{1,0:T(8,128)(2,1)}, u32[]{:S(2)}, u32[]{:S(2)}) collective-permute-start(bf16[512,512]{1,0:T(8,128)(2,1)} %get-tuple-element.206), channel_id=1, source_target_pairs={{0,4},{4,0},{8,12},{12,8},{1,5},{5,1},{9,13},{13,9},{2,6},{6,2},{1... | collective-permute-start | bytes 1572872 | tf_op jit(solution)/shard_map/ppermute | solution.py:59
  898.2 123.6 %collective-permute-start.25 = (bf16[512,512]{1,0:T(8,128)(2,1)}, bf16[512,512]{1,0:T(8,128)(2,1)}, u32[]{:S(2)}, u32[]{:S(2)}) collective-permute-start(bf16[512,512]{1,0:T(8,128)(2,1)} %get-tuple-element.194), channel_id=1, source_target_pairs={{0,4},{4,0},{8,12},{12,8},{1,5},{5,1},{9,13},{13,9},{2,6},{6,2},{1... | collective-permute-start | bytes 1572872 | tf_op jit(solution)/shard_map/ppermute | solution.py:59
  899.8 626.8 %collective-permute-start.15 = (bf16[512,512]{1,0:T(8,128)(2,1)}, bf16[512,512]{1,0:T(8,128)(2,1)}, u32[]{:S(2)}, u32[]{:S(2)}) collective-permute-start(bf16[512,512]{1,0:T(8,128)(2,1)} %get-tuple-element.200), channel_id=1, source_target_pairs={{0,4},{4,0},{8,12},{12,8},{1,5},{5,1},{9,13},{13,9},{2,6},{6,2},{1... | collective-permute-start | bytes 1572872 | tf_op jit(solution)/shard_map/ppermute | solution.py:59
  916.3 18.6 collective-permute-start.41
  936.7 80.7 %collective-permute-start.42 = (bf16[176,2048]{1,0:T(8,128)(2,1)}, bf16[176,2048]{1,0:T(8,128)(2,1)}, u32[]{:S(2)}, u32[]{:S(2)}) collective-permute-start(bf16[176,2048]{1,0:T(8,128)(2,1)} %pad_maximum_fusion.24), channel_id=1, source_target_pairs={{0,1},{1,0},{2,3},{3,2},{4,5},{5,4},{6,7},{7,6},{8,9},{9,8},{10,11... | collective-permute-start | bytes 2162696 | tf_op jit(solution)/shard_map/ppermute | solution.py:59
  1021.2 129.8 %collective-permute-start.43 = (bf16[352,2048]{1,0:T(8,128)(2,1)}, bf16[352,2048]{1,0:T(8,128)(2,1)}, u32[]{:S(2)}, u32[]{:S(2)}) collective-permute-start(bf16[352,2048]{1,0:T(8,128)(2,1)} %pad_maximum_fusion.19), channel_id=1, source_target_pairs={{0,16},{16,0},{1,17},{17,1},{2,18},{18,2},{3,19},{19,3},{4,20},{20... | collective-permute-start | bytes 4325384 | tf_op jit(solution)/shard_map/ppermute | solution.py:59
  1048.3 95.9 %collective-permute-start.28 = (bf16[256,5632]{1,0:T(8,128)(2,1)}, bf16[256,5632]{1,0:T(8,128)(2,1)}, u32[]{:S(2)}, u32[]{:S(2)}) collective-permute-start(bf16[256,5632]{1,0:T(8,128)(2,1)} %select_convert_fusion), channel_id=1, source_target_pairs={{0,16},{16,0},{1,17},{17,1},{2,18},{18,2},{3,19},{19,3},{4,20},{20... | collective-permute-start | bytes 8650760 | tf_op jit(solution)/shard_map/ppermute | solution.py:59
  1069.6 192.8 %all-to-all-start.3 = ((bf16[32,40,2048]{2,1,0:T(8,128)(2,1)}), bf16[32,40,2048]{2,1,0:T(8,128)(2,1)}, u32[]{:S(2)}, u32[]{:S(2)}) async-start(bf16[32,40,2048]{2,1,0:T(8,128)(2,1)} %bitcast.206), calls=%async_computation.3 | async-start | bytes 10485760 | tf_op jit(solution)/shard_map/all_to_all | solution.py:322
  1073.1 356.0 %reduce-scatter.2.cloned.1.call-start = ((), (), s32[]{:S(2)}) async-start(), calls=%async_computation.13 | async-start | bytes 1474560 | tf_op jit(solution)/shard_map/reduce_scatter | solution.py:387
  1150.9 45.9 %collective-permute-start.29 = (bf16[128,5632]{1,0:T(8,128)(2,1)S(1)}, bf16[128,5632]{1,0:T(8,128)(2,1)S(1)}, u32[]{:S(2)}, u32[]{:S(2)}) collective-permute-start(bf16[128,5632]{1,0:T(8,128)(2,1)S(1)} %select_convert_fusion.5), channel_id=1, source_target_pairs={{0,1},{1,0},{2,3},{3,2},{4,5},{5,4},{6,7},{7,6},{8,9},{9,8},{10,11... | collective-permute-start | bytes 4325384 | tf_op jit(solution)/shard_map/ppermute | solution.py:59
  1197.4 31.1 %collective-permute-start.30 = (bf16[64,5632]{1,0:T(8,128)(2,1)S(1)}, bf16[64,5632]{1,0:T(8,128)(2,1)S(1)}, u32[]{:S(2)}, u32[]{:S(2)}) collective-permute-start(bf16[64,5632]{1,0:T(8,128)(2,1)S(1)} %select_convert_fusion.10), channel_id=1, source_target_pairs={{0,2},{1,3},{2,0},{3,1},{4,6},{5,7},{6,4},{7,5},{8,10},{9,11},{10,... | collective-permute-start | bytes 2162696 | tf_op jit(solution)/shard_map/ppermute | solution.py:59
  1228.7 32.0 %collective-permute-start.31 = (bf16[64,5632]{1,0:T(8,128)(2,1)S(1)}, bf16[64,5632]{1,0:T(8,128)(2,1)S(1)}, u32[]{:S(2)}, u32[]{:S(2)}) collective-permute-start(bf16[64,5632]{1,0:T(8,128)(2,1)S(1)} %add_convert_fusion.1), channel_id=1, source_target_pairs={{0,2},{1,3},{2,0},{3,1},{4,6},{5,7},{6,4},{7,5},{8,10},{9,11},{10,... | collective-permute-start | bytes 2162696 | tf_op jit(solution)/shard_map/ppermute | solution.py:59
  1367.7 58.3 %collective-permute-start.16 = (bf16[256,2048]{1,0:T(8,128)(2,1)}, bf16[256,2048]{1,0:T(8,128)(2,1)}, u32[]{:S(2)}, u32[]{:S(2)}) collective-permute-start(bf16[256,2048]{1,0:T(8,128)(2,1)} %get-tuple-element.145), channel_id=1, source_target_pairs={{0,8},{4,12},{8,0},{12,4},{1,9},{5,13},{9,1},{13,5},{2,10},{6,14},... | collective-permute-start | bytes 3145736 | tf_op jit(solution)/shard_map/ppermute | solution.py:59
  1416.2 48.9 %collective-permute-start.4 = (bf16[256,4096]{1,0:T(8,128)(2,1)}, bf16[256,4096]{1,0:T(8,128)(2,1)}, u32[]{:S(2)}, u32[]{:S(2)}) collective-permute-start(bf16[256,4096]{1,0:T(8,128)(2,1)} %select_convert_fusion.3), channel_id=1, source_target_pairs={{0,8},{4,12},{8,0},{12,4},{1,9},{5,13},{9,1},{13,5},{2,10},{6,14},... | collective-permute-start | bytes 6291464 | tf_op jit(solution)/shard_map/ppermute | solution.py:59
  1429.2 97.6 %collective-permute-start.17 = (bf16[512,2048]{1,0:T(8,128)(2,1)}, bf16[512,2048]{1,0:T(8,128)(2,1)}, u32[]{:S(2)}, u32[]{:S(2)}) collective-permute-start(bf16[512,2048]{1,0:T(8,128)(2,1)} %pad_maximum_fusion.11), channel_id=1, source_target_pairs={{0,4},{4,0},{8,12},{12,8},{1,5},{5,1},{9,13},{13,9},{2,6},{6,2},{1... | collective-permute-start | bytes 6291464 | tf_op jit(solution)/shard_map/ppermute | solution.py:59
  1432.3 77.2 %collective-permute-start.2 = (bf16[256,3648]{0,1:T(8,128)(2,1)}, bf16[256,3648]{0,1:T(8,128)(2,1)}, u32[]{:S(2)}, u32[]{:S(2)}) collective-permute-start(bf16[256,3648]{0,1:T(8,128)(2,1)} %pad_maximum_fusion.13), channel_id=1, source_target_pairs={{0,8},{4,12},{8,0},{12,4},{1,9},{5,13},{9,1},{13,5},{2,10},{6,14},... | collective-permute-start | bytes 5603336 | tf_op jit(solution)/shard_map/ppermute | solution.py:59
  1465.1 44.4 %collective-permute-start.6 = (bf16[1024,19]{1,0:T(8,128)(2,1)S(1)}, bf16[1024,19]{1,0:T(8,128)(2,1)S(1)}, u32[]{:S(2)}, u32[]{:S(2)}) collective-permute-start(bf16[1024,19]{1,0:T(8,128)(2,1)S(1)} %select_convert_fusion.15), channel_id=1, source_target_pairs={{0,8},{4,12},{8,0},{12,4},{1,9},{5,13},{9,1},{13,5},{2,10},{6,14},... | collective-permute-start | bytes 116744 | tf_op jit(solution)/shard_map/ppermute | solution.py:59
  1519.7 17.5 collective-permute-start.3
  1519.8 6.6 collective-permute-start.7
  1526.5 8.5 collective-permute-start.5
  1526.6 48.1 %collective-permute-start.32 = (bf16[128,5632]{1,0:T(8,128)(2,1)}, bf16[128,5632]{1,0:T(8,128)(2,1)}, u32[]{:S(2)}, u32[]{:S(2)}) collective-permute-start(bf16[128,5632]{1,0:T(8,128)(2,1)} %pad_maximum_fusion.18), channel_id=1, source_target_pairs={{0,1},{1,0},{2,3},{3,2},{4,5},{5,4},{6,7},{7,6},{8,9},{9,8},{10,11... | collective-permute-start | bytes 4325384 | tf_op jit(solution)/shard_map/ppermute | solution.py:59
  1532.5 45.9 %collective-permute-start.18 = (bf16[256,2048]{1,0:T(8,128)(2,1)}, bf16[256,2048]{1,0:T(8,128)(2,1)}, u32[]{:S(2)}, u32[]{:S(2)}) collective-permute-start(bf16[256,2048]{1,0:T(8,128)(2,1)} %select_convert_fusion.7), channel_id=1, source_target_pairs={{0,16},{16,0},{1,17},{17,1},{2,18},{18,2},{3,19},{19,3},{4,20},{20... | collective-permute-start | bytes 3145736 | tf_op jit(solution)/shard_map/ppermute | solution.py:59
  1574.1 54.5 %collective-permute-start.8 = (bf16[256,4691]{0,1:T(8,128)(2,1)}, bf16[256,4691]{0,1:T(8,128)(2,1)}, u32[]{:S(2)}, u32[]{:S(2)}) collective-permute-start(bf16[256,4691]{0,1:T(8,128)(2,1)} %copy.184), channel_id=1, source_target_pairs={{0,16},{16,0},{1,17},{17,1},{2,18},{18,2},{3,19},{19,3},{4,20},{20... | collective-permute-start | bytes 7205384 | tf_op jit(solution)/shard_map/ppermute | solution.py:59
  1581.7 68.1 %collective-permute-start.19 = (bf16[128,2048]{1,0:T(8,128)(2,1)S(1)}, bf16[128,2048]{1,0:T(8,128)(2,1)}, u32[]{:S(2)}, u32[]{:S(2)}) collective-permute-start(bf16[128,2048]{1,0:T(8,128)(2,1)S(1)} %select_convert_fusion.12), channel_id=1, source_target_pairs={{0,1},{1,0},{2,3},{3,2},{4,5},{5,4},{6,7},{7,6},{8,9},{9,8},{10,11... | collective-permute-start | bytes 1572872 | tf_op jit(solution)/shard_map/ppermute | solution.py:59
  1643.9 33.5 %collective-permute-start.9 = (bf16[128,4691]{0,1:T(8,128)(2,1)}, bf16[128,4691]{0,1:T(8,128)(2,1)}, u32[]{:S(2)}, u32[]{:S(2)}) collective-permute-start(bf16[128,4691]{0,1:T(8,128)(2,1)} %copy.186), channel_id=1, source_target_pairs={{0,1},{1,0},{2,3},{3,2},{4,5},{5,4},{6,7},{7,6},{8,9},{9,8},{10,11... | collective-permute-start | bytes 3602696 | tf_op jit(solution)/shard_map/ppermute | solution.py:59
  1648.9 63.3 %collective-permute-start.33 = (bf16[256,5632]{1,0:T(8,128)(2,1)}, bf16[256,5632]{1,0:T(8,128)(2,1)}, u32[]{:S(2)}, u32[]{:S(2)}) collective-permute-start(bf16[256,5632]{1,0:T(8,128)(2,1)} %pad_maximum_fusion.7), channel_id=1, source_target_pairs={{0,16},{16,0},{1,17},{17,1},{2,18},{18,2},{3,19},{19,3},{4,20},{20... | collective-permute-start | bytes 8650760 | tf_op jit(solution)/shard_map/ppermute | solution.py:59
  1652.1 64.5 %collective-permute-start.20 = (bf16[64,2048]{1,0:T(8,128)(2,1)S(1)}, bf16[64,2048]{1,0:T(8,128)(2,1)S(1)}, u32[]{:S(2)}, u32[]{:S(2)}) collective-permute-start(bf16[64,2048]{1,0:T(8,128)(2,1)S(1)} %select_convert_fusion.14), channel_id=1, source_target_pairs={{0,2},{1,3},{2,0},{3,1},{4,6},{5,7},{6,4},{7,5},{8,10},{9,11},{10,... | collective-permute-start | bytes 786440 | tf_op jit(solution)/shard_map/ppermute | solution.py:59
  1683.1 35.2 %collective-permute-start.10 = (bf16[64,4691]{1,0:T(8,128)(2,1)S(1)}, bf16[64,4691]{1,0:T(8,128)(2,1)S(1)}, u32[]{:S(2)}, u32[]{:S(2)}) collective-permute-start(bf16[64,4691]{1,0:T(8,128)(2,1)S(1)} %select_convert_fusion.11), channel_id=1, source_target_pairs={{0,2},{1,3},{2,0},{3,1},{4,6},{5,7},{6,4},{7,5},{8,10},{9,11},{10,... | collective-permute-start | bytes 1801352 | tf_op jit(solution)/shard_map/ppermute | solution.py:59
  1716.7 26.0 %collective-permute-start.21 = (bf16[64,2048]{1,0:T(8,128)(2,1)S(1)}, bf16[64,2048]{1,0:T(8,128)(2,1)S(1)}, u32[]{:S(2)}, u32[]{:S(2)}) collective-permute-start(bf16[64,2048]{1,0:T(8,128)(2,1)S(1)} %add_convert_fusion.5), channel_id=1, source_target_pairs={{0,2},{1,3},{2,0},{3,1},{4,6},{5,7},{6,4},{7,5},{8,10},{9,11},{10,... | collective-permute-start | bytes 786440 | tf_op jit(solution)/shard_map/ppermute | solution.py:59
  1718.5 36.8 %collective-permute-start.11 = (bf16[64,4691]{1,0:T(8,128)(2,1)S(1)}, bf16[64,4691]{1,0:T(8,128)(2,1)S(1)}, u32[]{:S(2)}, u32[]{:S(2)}) collective-permute-start(bf16[64,4691]{1,0:T(8,128)(2,1)S(1)} %add_convert_fusion.2), channel_id=1, source_target_pairs={{0,2},{1,3},{2,0},{3,1},{4,6},{5,7},{6,4},{7,5},{8,10},{9,11},{10,... | collective-permute-start | bytes 1801352 | tf_op jit(solution)/shard_map/ppermute | solution.py:59
  1743.8 22.9 %collective-permute-start.22 = (bf16[128,2048]{1,0:T(8,128)(2,1)}, bf16[128,2048]{1,0:T(8,128)(2,1)}, u32[]{:S(2)}, u32[]{:S(2)}) collective-permute-start(bf16[128,2048]{1,0:T(8,128)(2,1)} %pad_maximum_fusion.30), channel_id=1, source_target_pairs={{0,1},{1,0},{2,3},{3,2},{4,5},{5,4},{6,7},{7,6},{8,9},{9,8},{10,11... | collective-permute-start | bytes 1572872 | tf_op jit(solution)/shard_map/ppermute | solution.py:59
  1757.2 35.1 %collective-permute-start.12 = (bf16[128,4691]{0,1:T(8,128)(2,1)}, bf16[128,4691]{0,1:T(8,128)(2,1)}, u32[]{:S(2)}, u32[]{:S(2)}) collective-permute-start(bf16[128,4691]{0,1:T(8,128)(2,1)} %copy.188), channel_id=1, source_target_pairs={{0,1},{1,0},{2,3},{3,2},{4,5},{5,4},{6,7},{7,6},{8,9},{9,8},{10,11... | collective-permute-start | bytes 3602696 | tf_op jit(solution)/shard_map/ppermute | solution.py:59
  1769.1 47.3 %collective-permute-start.23 = (bf16[256,2048]{1,0:T(8,128)(2,1)}, bf16[256,2048]{1,0:T(8,128)(2,1)}, u32[]{:S(2)}, u32[]{:S(2)}) collective-permute-start(bf16[256,2048]{1,0:T(8,128)(2,1)} %pad_maximum_fusion.22), channel_id=1, source_target_pairs={{0,16},{16,0},{1,17},{17,1},{2,18},{18,2},{3,19},{19,3},{4,20},{20... | collective-permute-start | bytes 3145736 | tf_op jit(solution)/shard_map/ppermute | solution.py:59
  1803.3 54.5 %collective-permute-start.13 = (bf16[256,4691]{0,1:T(8,128)(2,1)}, bf16[256,4691]{0,1:T(8,128)(2,1)}, u32[]{:S(2)}, u32[]{:S(2)}) collective-permute-start(bf16[256,4691]{0,1:T(8,128)(2,1)} %copy.191), channel_id=1, source_target_pairs={{0,16},{16,0},{1,17},{17,1},{2,18},{18,2},{3,19},{19,3},{4,20},{20... | collective-permute-start | bytes 7205384 | tf_op jit(solution)/shard_map/ppermute | solution.py:59
  (124 other events, 1368.4 us)
Sparse Core Ops, SparseCore 0:
  9.6 26.7 all-gather.14
  41.3 31.7 all-gather.16
  74.6 32.8 all-gather.18
  108.9 82.0 all-gather.20
  192.4 58.2 all-gather.22
  252.2 127.6 all-gather.24
  381.5 122.9 all-gather.26
  506.0 83.4 all-gather.28
  1392.2 29.2 reduce-scatter.1

commit v2 on v1

--- a/solution.py
+++ b/solution.py
@@ -1,6 +1,10 @@
+import functools
+
 import jax
 import jax.numpy as jnp
 from jax import lax
+from jax.experimental import pallas as pl
+from jax.experimental.pallas import tpu as pltpu
 from jax.sharding import PartitionSpec as P
 
 D = 2048
@@ -110,8 +114,490 @@
     return values.astype(jnp.float32)
 
 
-def total(values):
-    return jnp.sum(lax.all_gather(values, ("replica", "fsdp", "ctx"), axis=0, tiled=True))
+def total(value):
+    spread = jnp.full((8, 128), value, jnp.float32)
+    for axis in ("fsdp", "replica", "ctx"):
+        for mask in masks(lax.axis_size(axis)):
+            spread = spread + swap(spread, axis, mask)
+    return spread[0, 0]
+
+
+def column_dot(first_mat, second_mat):
+    return lax.dot_general(
+        first_mat, second_mat, (((0,), (0,)), ((), ())), preferred_element_type=jnp.float32
+    )
+
+
+def turned_query(q_ref, cos_ref, sin_ref, head):
+    start = head * (NOPE + ROPE)
+    flat = q_ref[:, start : start + NOPE].astype(jnp.bfloat16)
+    first = q_ref[:, start + NOPE : start + NOPE + ROPE // 2]
+    second = q_ref[:, start + NOPE + ROPE // 2 : start + NOPE + ROPE]
+    cosine, sine_part = cos_ref[...], sin_ref[...]
+    turned = jnp.concatenate(
+        [first * cosine - second * sine_part, first * sine_part + second * cosine], axis=1
+    ).astype(jnp.bfloat16)
+    return flat, turned
+
+
+PAIR = 2
+
+
+def attention_kernel(q_ref, e_ref, rope_ref, cos_ref, sin_ref, kb_ref, qb_ref, out_ref):
+    allowed = kb_ref[...] <= qb_ref[...]
+    for head in range(PAIR):
+        flat, turned = turned_query(q_ref, cos_ref, sin_ref, head)
+        at = head * (NOPE + VDIM)
+        scores = (
+            cols_dot(flat, e_ref[:, at : at + NOPE]) + cols_dot(turned, rope_ref[...])
+        ) * (NOPE + ROPE) ** (-0.5)
+        scores = jnp.where(allowed, scores, -1e30)
+        weights = jnp.exp(scores - jnp.max(scores, axis=1, keepdims=True))
+        probs = weights * (1.0 / jnp.sum(weights, axis=1, keepdims=True))
+        out_ref[:, head * VDIM : (head + 1) * VDIM] = matmul(
+            probs.astype(jnp.bfloat16), e_ref[:, at + NOPE : at + NOPE + VDIM]
+        ).astype(jnp.bfloat16)
+
+
+def attention_back_kernel(
+    q_ref, e_ref, rope_ref, cos_ref, sin_ref, kb_ref, qb_ref, ga_ref, gq_ref, ge_ref, gr_ref
+):
+    @pl.when(pl.program_id(0) == 0)
+    def _():
+        gr_ref[...] = jnp.zeros_like(gr_ref)
+
+    allowed = kb_ref[...] <= qb_ref[...]
+    scale = (NOPE + ROPE) ** (-0.5)
+    cosine, sine_part = cos_ref[...], sin_ref[...]
+    for head in range(PAIR):
+        flat, turned = turned_query(q_ref, cos_ref, sin_ref, head)
+        at = head * (NOPE + VDIM)
+        key_flat, value = e_ref[:, at : at + NOPE], e_ref[:, at + NOPE : at + NOPE + VDIM]
+        grad_att = ga_ref[:, head * VDIM : (head + 1) * VDIM]
+        scores = (cols_dot(key_flat, flat) + cols_dot(rope_ref[...], turned)) * scale
+        scores = jnp.where(allowed, scores, -1e30)
+        weights = jnp.exp(scores - jnp.max(scores, axis=0, keepdims=True))
+        probs = weights * (1.0 / jnp.sum(weights, axis=0, keepdims=True))
+        grad_value = matmul(probs.astype(jnp.bfloat16), grad_att)
+        grad_probs = cols_dot(value, grad_att)
+        row_dot = jnp.sum(probs * grad_probs, axis=0, keepdims=True)
+        grad_scores = (probs * (grad_probs - row_dot)).astype(jnp.bfloat16)
+        ge_ref[:, at : at + NOPE] = (matmul(grad_scores, flat) * scale).astype(jnp.bfloat16)
+        ge_ref[:, at + NOPE : at + NOPE + VDIM] = grad_value.astype(jnp.bfloat16)
+        gr_ref[...] += matmul(grad_scores, turned) * scale
+        grad_flat = column_dot(grad_scores, key_flat) * scale
+        grad_turned = column_dot(grad_scores, rope_ref[...]) * scale
+        first, second = grad_turned[:, : ROPE // 2], grad_turned[:, ROPE // 2 :]
+        start = head * (NOPE + ROPE)
+        gq_ref[:, start : start + NOPE + ROPE] = jnp.concatenate(
+            [
+                grad_flat,
+                first * cosine + second * sine_part,
+                second * cosine - first * sine_part,
+            ],
+            axis=1,
+        ).astype(jnp.bfloat16)
+
+
+def whole(shape):
+    return pl.BlockSpec(shape, lambda i: (0, 0))
+
+
+def attention(query_raw, expanded, rope_all, cosine, sine_part, key_block, query_block):
+    rows, keys = query_raw.shape[0], expanded.shape[0]
+    return pl.pallas_call(
+        attention_kernel,
+        grid=(HEADS // PAIR,),
+        in_specs=[
+            pl.BlockSpec((rows, PAIR * (NOPE + ROPE)), lambda i: (0, i)),
+            pl.BlockSpec((keys, PAIR * (NOPE + VDIM)), lambda i: (0, i)),
+            whole((keys, ROPE)),
+            whole((rows, ROPE // 2)),
+            whole((rows, ROPE // 2)),
+            whole((1, keys)),
+            whole((rows, 1)),
+        ],
+        out_specs=pl.BlockSpec((rows, PAIR * VDIM), lambda i: (0, i)),
+        out_shape=jax.ShapeDtypeStruct((rows, HEADS * VDIM), jnp.bfloat16),
+        compiler_params=pltpu.CompilerParams(vmem_limit_bytes=40 * 1024 * 1024),
+        cost_estimate=pl.CostEstimate(
+            flops=2 * rows * keys * HEADS * (NOPE + ROPE + VDIM),
+            bytes_accessed=12 * 1024 * 1024,
+            transcendentals=rows * keys * HEADS,
+        ),
+        name="attention",
+    )(
+        query_raw,
+        expanded,
+        rope_all,
+        cosine,
+        sine_part,
+        key_block.reshape(1, keys),
+        query_block.reshape(rows, 1),
+    )
+
+
+def attention_back(
+    query_raw, expanded, rope_all, cosine, sine_part, key_block, query_block, grad_att
+):
+    rows, keys = query_raw.shape[0], expanded.shape[0]
+    return pl.pallas_call(
+        attention_back_kernel,
+        grid=(HEADS // PAIR,),
+        in_specs=[
+            pl.BlockSpec((rows, PAIR * (NOPE + ROPE)), lambda i: (0, i)),
+            pl.BlockSpec((keys, PAIR * (NOPE + VDIM)), lambda i: (0, i)),
+            whole((keys, ROPE)),
+            whole((rows, ROPE // 2)),
+            whole((rows, ROPE // 2)),
+            whole((keys, 1)),
+            whole((1, rows)),
+            pl.BlockSpec((rows, PAIR * VDIM), lambda i: (0, i)),
+        ],
+        out_specs=(
+            pl.BlockSpec((rows, PAIR * (NOPE + ROPE)), lambda i: (0, i)),
+            pl.BlockSpec((keys, PAIR * (NOPE + VDIM)), lambda i: (0, i)),
+            whole((keys, ROPE)),
+        ),
+        out_shape=(
+            jax.ShapeDtypeStruct((rows, HEADS * (NOPE + ROPE)), jnp.bfloat16),
+            jax.ShapeDtypeStruct((keys, HEADS * (NOPE + VDIM)), jnp.bfloat16),
+            jax.ShapeDtypeStruct((keys, ROPE), jnp.float32),
+        ),
+        compiler_params=pltpu.CompilerParams(vmem_limit_bytes=40 * 1024 * 1024),
+        cost_estimate=pl.CostEstimate(
+            flops=2 * rows * keys * HEADS * (3 * (NOPE + ROPE) + 2 * VDIM),
+            bytes_accessed=24 * 1024 * 1024,
+            transcendentals=rows * keys * HEADS,
+        ),
+        name="attention_back",
+    )(
+        query_raw,
+        expanded,
+        rope_all,
+        cosine,
+        sine_part,
+        key_block.reshape(keys, 1),
+        query_block.reshape(1, rows),
+        grad_att,
+    )
+
+
+MESH = pl.DeviceIdType.MESH
+STEP = 8
+
+
+def rows_of(ref, first, count):
+    block = ref[pl.ds(first, count)].astype(jnp.float32)
+    return block.reshape(count * block.shape[1], block.shape[2]).astype(jnp.bfloat16)
+
+
+def put_rows(ref, first, count, rows):
+    ref[pl.ds(first, count)] = rows.reshape(count, ref.shape[1], ref.shape[2]).astype(ref.dtype)
+
+
+def exchange(send, arrived, part, back, xin, ret, sems, group, prepare):
+    n, step = send.shape[0], STEP
+    local_sem, ssem, rsem, fsem, gsem, psem, qsem, bsem, tsem = sems
+    columns = lax.axis_size("ctx")
+    me = lax.axis_index("fsdp") * columns + lax.axis_index("ctx")
+    other = {"replica": 1 - lax.axis_index("replica")}
+
+    def place(index):
+        return {"fsdp": index // columns, "ctx": index % columns}
+
+    def dispatch(slot):
+        to = (me + slot) % n
+        return pltpu.make_async_remote_copy(
+            src_ref=send.at[to],
+            dst_ref=arrived.at[slot],
+            send_sem=ssem.at[slot],
+            recv_sem=rsem.at[slot],
+            device_id=place(to),
+            device_id_type=MESH,
+        )
+
+    def forward(slot):
+        return pltpu.make_async_remote_copy(
+            src_ref=arrived.at[slot],
+            dst_ref=arrived.at[n + slot],
+            send_sem=fsem.at[slot],
+            recv_sem=gsem.at[slot],
+            device_id=other,
+            device_id_type=MESH,
+        )
+
+    def across(slot):
+        return pltpu.make_async_remote_copy(
+            src_ref=part.at[n + slot],
+            dst_ref=xin.at[slot],
+            send_sem=psem.at[slot],
+            recv_sem=qsem.at[slot],
+            device_id=other,
+            device_id_type=MESH,
+        )
+
+    def give_back(slot, from_index):
+        return pltpu.make_async_remote_copy(
+            src_ref=back.at[slot],
+            dst_ref=ret.at[from_index],
+            send_sem=bsem.at[slot],
+            recv_sem=tsem.at[slot],
+            device_id=place((me + n - slot) % n),
+            device_id_type=MESH,
+        )
+
+    barrier = pltpu.get_barrier_semaphore()
+
+    @pl.loop(1, n)
+    def _(slot):
+        pl.semaphore_signal(
+            barrier, inc=1, device_id=place((me + slot) % n), device_id_type=MESH
+        )
+
+    pl.semaphore_signal(barrier, inc=1, device_id=other, device_id_type=MESH)
+    pl.semaphore_wait(barrier, n)
+
+    own = pltpu.make_async_copy(send.at[me], arrived.at[0], local_sem.at[0])
+    own.start()
+
+    @pl.loop(1, n)
+    def _(slot):
+        dispatch(slot).start()
+
+    own.wait()
+    forward(0).start()
+    prepare()
+
+    @pl.loop(0, n // step)
+    def _(turn):
+        @pl.loop(0, step)
+        def _(i):
+            slot = turn * step + i
+
+            @pl.when(slot > 0)
+            def _():
+                dispatch(slot).wait_recv()
+                forward(slot).start()
+
+        group(turn * step)
+
+    @pl.loop(0, n // step)
+    def _(turn):
+        @pl.loop(0, step)
+        def _(i):
+            forward(turn * step + i).wait_recv()
+
+        group(n + turn * step)
+
+        @pl.loop(0, step)
+        def _(i):
+            across(turn * step + i).start()
+
+    @pl.loop(0, n)
+    def _(slot):
+        across(slot).wait_recv()
+        back[pl.ds(slot, 1)] = (
+            part[pl.ds(slot, 1)].astype(jnp.float32) + xin[pl.ds(slot, 1)].astype(jnp.float32)
+        ).astype(jnp.bfloat16)
+
+        @pl.when(slot > 0)
+        def _():
+            give_back(slot, me).start()
+
+    keep = pltpu.make_async_copy(back.at[0], ret.at[me], local_sem.at[0])
+    keep.start()
+    keep.wait()
+
+    @pl.loop(1, n)
+    def _(slot):
+        dispatch(slot).wait_send()
+        give_back(slot, (me + slot) % n).wait()
+
+    @pl.loop(0, n)
+    def _(slot):
+        forward(slot).wait_send()
+        across(slot).wait_send()
+
+
+def experts_kernel(
+    send, gate, up, down, kept, ret, w_gate, w_up, w_down, arrived, part, back, xin, wsem, *sems
+):
+    n = send.shape[0]
+    loads = [
+        pltpu.make_async_copy(source, target, wsem.at[i])
+        for i, (source, target) in enumerate(((gate, w_gate), (up, w_up), (down, w_down)))
+    ]
+
+    def prepare():
+        for load in loads:
+            load.wait()
+
+    def group(first):
+        rows = rows_of(arrived, first, STEP)
+        gate_in = matmul(rows, w_gate[...])
+        act = (gate_in * jax.nn.sigmoid(gate_in) * matmul(rows, w_up[...])).astype(jnp.bfloat16)
+        put_rows(part, first, STEP, matmul(act, w_down[...]))
+
+    for load in loads:
+        load.start()
+    exchange(send, arrived, part, back, xin, ret, sems, group, prepare)
+    save = pltpu.make_async_copy(arrived, kept, wsem.at[0])
+    save.start()
+    save.wait()
+
+
+def experts_back_kernel(
+    send,
+    rows_in,
+    gate,
+    up,
+    down,
+    kept,
+    act_out,
+    gg_out,
+    gu_out,
+    ret,
+    w_gate,
+    w_up,
+    w_down,
+    rows_kept,
+    slope,
+    silu,
+    arrived,
+    part,
+    back,
+    xin,
+    wsem,
+    *sems,
+):
+    n = send.shape[0]
+    loads = [
+        pltpu.make_async_copy(source, target, wsem.at[i])
+        for i, (source, target) in enumerate(
+            ((rows_in, rows_kept), (gate, w_gate), (up, w_up), (down, w_down))
+        )
+    ]
+    size = STEP * send.shape[1]
+
+    def prepare():
+        for load in loads:
+            load.wait()
+
+        @pl.loop(0, 2 * n // STEP)
+        def _(turn):
+            rows = rows_of(rows_kept, turn * STEP, STEP)
+            at = pl.ds(pl.multiple_of(turn * size, size), size)
+            gate_in = matmul(rows, w_gate[...])
+            up_in = matmul(rows, w_up[...])
+            sigmoid = jax.nn.sigmoid(gate_in)
+            silu_in = gate_in * sigmoid
+            silu[at] = silu_in
+            slope[at] = up_in * silu_slope(gate_in, sigmoid)
+            act_out[at] = (silu_in * up_in).astype(jnp.bfloat16)
+
+    def group(first):
+        grads = rows_of(arrived, first, STEP)
+        at = pl.ds(pl.multiple_of(first * send.shape[1], size), size)
+        grad_act = cols_dot(grads, w_down[...])
+        grad_gate_in = (grad_act * slope[at]).astype(jnp.bfloat16)
+        grad_up_in = (grad_act * silu[at]).astype(jnp.bfloat16)
+        gg_out[at] = grad_gate_in
+        gu_out[at] = grad_up_in
+        put_rows(
+            part,
+            first,
+            STEP,
+            cols_dot(grad_gate_in, w_gate[...]) + cols_dot(grad_up_in, w_up[...]),
+        )
+
+    for load in loads:
+        load.start()
+    exchange(send, arrived, part, back, xin, ret, sems, group, prepare)
+    save = pltpu.make_async_copy(arrived, kept, wsem.at[0])
+    save.start()
+    save.wait()
+
+
+def exchange_scratch(n, cap, width):
+    return [
+        pltpu.VMEM((2 * n, cap, width), jnp.bfloat16),
+        pltpu.VMEM((2 * n, cap, width), jnp.bfloat16),
+        pltpu.VMEM((n, cap, width), jnp.bfloat16),
+        pltpu.VMEM((n, cap, width), jnp.bfloat16),
+        pltpu.SemaphoreType.DMA((4,)),
+        pltpu.SemaphoreType.DMA((1,)),
+    ] + [pltpu.SemaphoreType.DMA((n,)) for _ in range(8)]
+
+
+def any_spec():
+    return pl.BlockSpec(memory_space=pl.ANY)
+
+
+def experts(send, gate, up, down):
+    n, cap, width = send.shape
+    hidden = gate.shape[1]
+    return pl.pallas_call(
+        experts_kernel,
+        in_specs=[any_spec()] * 4,
+        out_specs=(any_spec(), any_spec()),
+        out_shape=(
+            jax.ShapeDtypeStruct((2 * n, cap, width), jnp.bfloat16),
+            jax.ShapeDtypeStruct((n, cap, width), jnp.bfloat16),
+        ),
+        scratch_shapes=[
+            pltpu.VMEM((width, hidden), jnp.bfloat16),
+            pltpu.VMEM((width, hidden), jnp.bfloat16),
+            pltpu.VMEM((hidden, width), jnp.bfloat16),
+        ]
+        + exchange_scratch(n, cap, width),
+        compiler_params=pltpu.CompilerParams(
+            collective_id=0, has_side_effects=True, vmem_limit_bytes=60 * 1024 * 1024
+        ),
+        cost_estimate=pl.CostEstimate(
+            flops=2 * 2 * n * cap * width * hidden * 3,
+            bytes_accessed=400 * 1024 * 1024,
+            transcendentals=2 * n * cap * hidden,
+        ),
+        name="experts",
+    )(send, gate, up, down)
+
+
+def experts_back(send, rows, gate, up, down):
+    n, cap, width = send.shape
+    hidden = gate.shape[1]
+    vmem = pl.BlockSpec(memory_space=pltpu.VMEM)
+    hidden_rows = jax.ShapeDtypeStruct((2 * n * cap, hidden), jnp.bfloat16)
+    return pl.pallas_call(
+        experts_back_kernel,
+        in_specs=[any_spec()] * 5,
+        out_specs=(any_spec(), vmem, vmem, vmem, any_spec()),
+        out_shape=(
+            jax.ShapeDtypeStruct((2 * n, cap, width), jnp.bfloat16),
+            hidden_rows,
+            hidden_rows,
+            hidden_rows,
+            jax.ShapeDtypeStruct((n, cap, width), jnp.bfloat16),
+        ),
+        scratch_shapes=[
+            pltpu.VMEM((width, hidden), jnp.bfloat16),
+            pltpu.VMEM((width, hidden), jnp.bfloat16),
+            pltpu.VMEM((hidden, width), jnp.bfloat16),
+            pltpu.VMEM((2 * n, cap, width), jnp.bfloat16),
+            pltpu.VMEM((2 * n * cap, hidden), jnp.float32),
+            pltpu.VMEM((2 * n * cap, hidden), jnp.float32),
+        ]
+        + exchange_scratch(n, cap, width),
+        compiler_params=pltpu.CompilerParams(
+            collective_id=1, has_side_effects=True, vmem_limit_bytes=63 * 1024 * 1024
+        ),
+        cost_estimate=pl.CostEstimate(
+            flops=2 * 2 * n * cap * width * hidden * 5,
+            bytes_accessed=400 * 1024 * 1024,
+            transcendentals=2 * n * cap * hidden,
+        ),
+        name="experts_back",
+    )(send, rows, gate, up, down)
 
 
 def per_device(
@@ -135,7 +621,6 @@
     expert_up,
     expert_down,
 ):
-    rep_count = lax.axis_size("replica")
     rows_dev = hidden_in.shape[1]
     offset = lax.axis_index("ctx") * rows_dev
     resid = hidden_in.reshape(rows_dev, D).astype(jnp.float32)
@@ -145,15 +630,25 @@
     query_block = lax.dynamic_slice_in_dim(key_block, offset, rows_dev)
     route_ids = routes.reshape(rows_dev, routes.shape[-1])
     top_count = route_ids.shape[1]
-    gain_one, query_mat, latent_mat, gain_latent, expand_mat, out_mat = (
-        lax.all_gather(attn_gain, "fsdp", axis=0, tiled=True),
+    fsdp_count = lax.axis_size("fsdp")
+    gain_rows, latent_rows = attn_gain.shape[0], latent_gain.shape[0]
+    small_all = lax.all_gather(
+        jnp.concatenate([attn_gain, ffn_gain, latent_gain, w_router.reshape(-1)])[None],
+        "fsdp",
+        axis=0,
+        tiled=True,
+    )
+    gain_one = small_all[:, :gain_rows].reshape(D)
+    gain_two = small_all[:, gain_rows : 2 * gain_rows].reshape(D)
+    gain_latent = small_all[:, 2 * gain_rows : 2 * gain_rows + latent_rows].reshape(LATENT)
+    router_mat = small_all[:, 2 * gain_rows + latent_rows :].reshape(D, w_router.shape[1])
+    query_mat, latent_mat, expand_mat, out_mat = (
         lax.all_gather(w_query, "fsdp", axis=0, tiled=True),
         lax.all_gather(w_latent, "fsdp", axis=0, tiled=True),
-        lax.all_gather(latent_gain, "fsdp", axis=0, tiled=True),
         lax.all_gather(w_expand, "fsdp", axis=0, tiled=True),
         lax.all_gather(w_out, "fsdp", axis=0, tiled=True),
     )
-    valid_count = total(valid_mask).astype(jnp.float32)
+    valid_count = total(jnp.sum(valid_rows))
     gain_one = gain_one.astype(jnp.float32)
     gain_latent = gain_latent.astype(jnp.float32)
     positions = (offset + jnp.arange(rows_dev)).astype(jnp.float32)
@@ -162,17 +657,11 @@
     cosine = jnp.cos(phase)
     sine_part = jnp.sin(phase)
 
-    def turn_query(values):
-        return rotate(values, cosine[:, None, :], sine_part[:, None, :])
-
     def turn_key(values):
         return rotate(values, cosine, sine_part)
 
     normed = rms_norm(resid, gain_one).astype(jnp.bfloat16)
-    query_raw = matmul(normed, query_mat).reshape(rows_dev, HEADS, NOPE + ROPE)
-    query_rot = jnp.concatenate(
-        [query_raw[..., :NOPE], turn_query(query_raw[..., NOPE:])], axis=-1
-    ).astype(jnp.bfloat16)
+    query_raw = matmul(normed, query_mat)
     latent_raw = matmul(normed, latent_mat)
     latent_part = latent_raw[:, :LATENT]
     rope_part = latent_raw[:, LATENT:]
@@ -182,38 +671,12 @@
         jnp.concatenate([latent_own, rope_own], axis=1), "ctx", axis=0, tiled=True
     )
     latent_all, rope_all = latent_rope[:, :LATENT], latent_rope[:, LATENT:]
-    key_count = latent_all.shape[0]
-    expanded = (
-        matmul(latent_all, expand_mat).astype(jnp.bfloat16).reshape(key_count, HEADS, NOPE + VDIM)
-    )
-    key_full = jnp.concatenate(
-        [expanded[..., :NOPE], jnp.broadcast_to(rope_all[:, None, :], (key_count, HEADS, ROPE))],
-        axis=-1,
-    )
-    value_rows = expanded[..., NOPE:]
-    score_scale = (NOPE + ROPE) ** (-0.5)
-    allowed = key_block[None, :] <= query_block[:, None]
-
-    def score_rows():
-        raw_scores = (
-            jnp.einsum("qhd,khd->hqk", query_rot, key_full, preferred_element_type=jnp.float32)
-            * score_scale
-        )
-        return jnp.where(allowed[None], raw_scores, -1e30)
-
-    scores = score_rows()
-    peak = jnp.max(scores, axis=-1, keepdims=True)
-    log_total = peak + jnp.log(jnp.sum(jnp.exp(scores - peak), axis=-1, keepdims=True))
-    attn_probs = jnp.exp(scores - log_total).astype(jnp.bfloat16)
-    attended = (
-        jnp.einsum("hqk,khv->qhv", attn_probs, value_rows, preferred_element_type=jnp.float32)
-        .reshape(rows_dev, HEADS * VDIM)
-        .astype(jnp.bfloat16)
+    expanded = matmul(latent_all, expand_mat).astype(jnp.bfloat16)
+    attended = attention(
+        query_raw, expanded, rope_all, cosine, sine_part, key_block, query_block
     )
     mixed = resid + matmul(attended, out_mat)
-    gain_two, router_mat, share_gate_mat, share_up_mat, share_down_mat = (
-        lax.all_gather(ffn_gain, "fsdp", axis=0, tiled=True),
-        lax.all_gather(w_router, "fsdp", axis=0, tiled=True),
+    share_gate_mat, share_up_mat, share_down_mat = (
         lax.all_gather(shared_gate, "fsdp", axis=0, tiled=True),
         lax.all_gather(shared_up, "fsdp", axis=0, tiled=True),
         lax.all_gather(shared_down, "fsdp", axis=0, tiled=True),
@@ -232,6 +695,7 @@
     share_act = (share_gate_in * share_sig * share_up_in).astype(jnp.bfloat16)
     share_out = matmul(share_act, share_down_mat)
     capacity = 5 * rows_dev * top_count // (4 * expert_count)
+    capacity = (capacity + 7) // 8 * 8
     flat_ids = route_ids.reshape(-1)
     hits = (flat_ids[:, None] == expert_ids[None, :]).astype(jnp.int32)
     ranks = jnp.sum((jnp.cumsum(hits, axis=0) - hits) * hits, axis=1)
@@ -244,39 +708,17 @@
     )
     padded = jnp.concatenate([normed_two, jnp.zeros((1, D), jnp.bfloat16)], axis=0)
     send_rows = jnp.take(padded, owner, axis=0)
-    payload = jnp.broadcast_to(send_rows[None], (rep_count, expert_count * capacity, D)).reshape(
-        rep_count * expert_count, capacity, D
-    )
     own_gate = expert_gate[0]
     own_up = expert_up[0]
     own_down = expert_down[0]
-    arrived = lax.all_to_all(
-        payload, ("replica", "fsdp", "ctx"), split_axis=0, concat_axis=0, tiled=True
-    )
-    source_count, item_count, _ = arrived.shape
-    flat_rows = arrived.reshape(source_count * item_count, D)
-    gate_in = matmul(flat_rows, own_gate)
-    up_in = matmul(flat_rows, own_up)
-    act_rows = (gate_in * jax.nn.sigmoid(gate_in) * up_in).astype(jnp.bfloat16)
-    partial_out = (
-        matmul(act_rows, own_down).astype(jnp.bfloat16).reshape(source_count, item_count, D)
-    )
-    returned = lax.all_to_all(
-        partial_out, ("replica", "fsdp", "ctx"), split_axis=0, concat_axis=0, tiled=True
-    )
-    returned, received = (returned, arrived)
-    slot_out = jnp.sum(
-        returned.astype(jnp.float32).reshape(rep_count, expert_count * capacity, D), axis=0
-    )
+    received, returned = experts(
+        send_rows.reshape(expert_count, capacity, D), own_gate, own_up, own_down
+    )
+    slot_out = returned.reshape(expert_count * capacity, D).astype(jnp.float32)
     picked = jnp.take(slot_out, slots, axis=0).reshape(rows_dev, top_count, D)
     final = mixed + share_out + jnp.sum(gates[:, :, None] * picked, axis=1)
     error_rows = final - target
-    error_total = total(
-        jnp.sum(
-            (valid_rows[:, None] * error_rows * error_rows).reshape(rows_dev, D // 128, 128),
-            axis=(0, 1),
-        )[None]
-    )
+    error_total = total(jnp.sum(valid_rows[:, None] * error_rows * error_rows))
     loss_value = error_total / (valid_count * D)
     grad_final = 2.0 / (valid_count * D) * valid_rows[:, None] * error_rows
     grad_gate = jnp.sum(picked * grad_final[:, None, :], axis=-1)
@@ -293,38 +735,15 @@
     slot_grads = jnp.take(
         jnp.concatenate([row_grads, jnp.zeros((1, D), jnp.float32)], axis=0), slot_source, axis=0
     ).astype(jnp.bfloat16)
-    grad_payload = jnp.broadcast_to(
-        slot_grads[None], (rep_count, expert_count * capacity, D)
-    ).reshape(rep_count * expert_count, capacity, D)
-    grad_in = lax.all_to_all(
-        grad_payload, ("replica", "fsdp", "ctx"), split_axis=0, concat_axis=0, tiled=True
+    grad_in, act_again, grad_gate_in, grad_up_in, grad_back = experts_back(
+        slot_grads.reshape(expert_count, capacity, D), received, own_gate, own_up, own_down
     )
     rows_flat = received.reshape(-1, D)
     grads_flat = grad_in.reshape(-1, D)
-    gate_again = matmul(rows_flat, own_gate)
-    up_again = matmul(rows_flat, own_up)
-    sigmoid_again = jax.nn.sigmoid(gate_again)
-    silu_again = gate_again * sigmoid_again
-    act_again = (silu_again * up_again).astype(jnp.bfloat16)
     expert_down_grad = rows_dot(act_again, grads_flat)
-    grad_act = cols_dot(grads_flat, own_down)
-    grad_gate_in = (grad_act * up_again * silu_slope(gate_again, sigmoid_again)).astype(
-        jnp.bfloat16
-    )
-    grad_up_in = (grad_act * silu_again).astype(jnp.bfloat16)
     expert_gate_grad = rows_dot(rows_flat, grad_gate_in)
     expert_up_grad = rows_dot(rows_flat, grad_up_in)
-    grad_rows = (
-        (cols_dot(grad_gate_in, own_gate) + cols_dot(grad_up_in, own_up))
-        .astype(jnp.bfloat16)
-        .reshape(received.shape)
-    )
-    grad_back = lax.all_to_all(
-        grad_rows, ("replica", "fsdp", "ctx"), split_axis=0, concat_axis=0, tiled=True
-    )
-    grad_slots = jnp.sum(
-        grad_back.astype(jnp.float32).reshape(rep_count, expert_count * capacity, D), axis=0
-    )
+    grad_slots = grad_back.reshape(expert_count * capacity, D).astype(jnp.float32)
     grad_normed_two = jnp.sum(
         jnp.take(grad_slots, slots, axis=0).reshape(rows_dev, top_count, D), axis=1
     )
@@ -358,32 +777,12 @@
     grad_mixed = grad_final + grad_mixed_norm
     grad_mix = grad_mixed.astype(jnp.bfloat16)
     g_out = sum_rows(rows_dot(own_columns(attended), gather_tokens(grad_mix)))
-    grad_att = cols_dot(grad_mix, out_mat).astype(jnp.bfloat16).reshape(rows_dev, HEADS, VDIM)
-    scores = score_rows()
-    prob_rows = jnp.exp(scores - log_total)
-    prob_low = prob_rows.astype(jnp.bfloat16)
-    grad_value = jnp.einsum("hqk,qhv->khv", prob_low, grad_att, preferred_element_type=jnp.float32)
-    grad_probs = jnp.einsum(
-        "qhv,khv->hqk", grad_att, value_rows, preferred_element_type=jnp.float32
-    )
-    row_dot = jnp.sum(prob_rows * grad_probs, axis=-1, keepdims=True)
-    grad_scores = (prob_rows * (grad_probs - row_dot)).astype(jnp.bfloat16)
-    grad_query = (
-        jnp.einsum("hqk,khd->qhd", grad_scores, key_full, preferred_element_type=jnp.float32)
-        * score_scale
-    )
-    grad_key = (
-        jnp.einsum("hqk,qhd->khd", grad_scores, query_rot, preferred_element_type=jnp.float32)
-        * score_scale
-    )
-    grad_expanded = (
-        jnp.concatenate([grad_key[..., :NOPE], grad_value], axis=-1)
-        .astype(jnp.bfloat16)
-        .reshape(key_count, HEADS * (NOPE + VDIM))
+    grad_att = cols_dot(grad_mix, out_mat).astype(jnp.bfloat16)
+    grad_query_raw, grad_expanded, grad_rope_all = attention_back(
+        query_raw, expanded, rope_all, cosine, sine_part, key_block, query_block, grad_att
     )
     full_expand = rows_dot(latent_all, grad_expanded)
     grad_latent_all = cols_dot(grad_expanded, expand_mat)
-    grad_rope_all = jnp.sum(grad_key[..., NOPE:], axis=1)
     grad_latent_rope = lax.psum_scatter(
         jnp.concatenate([grad_latent_all, grad_rope_all], axis=1).astype(jnp.bfloat16),
         "ctx",
@@ -398,13 +797,6 @@
     grad_latent_raw = jnp.concatenate([grad_latent_part, grad_rope_raw], axis=-1).astype(
         jnp.bfloat16
     )
-    _, query_back = jax.vjp(turn_query, query_raw[..., NOPE:])
-    (grad_query_rope,) = query_back(grad_query[..., NOPE:])
-    grad_query_raw = (
-        jnp.concatenate([grad_query[..., :NOPE], grad_query_rope], axis=-1)
-        .astype(jnp.bfloat16)
-        .reshape(rows_dev, HEADS * (NOPE + ROPE))
-    )
     query_width = grad_query_raw.shape[1]
     own_first = rows_dot(
         own_columns(normed),
@@ -414,7 +806,6 @@
     _, norm_one_back = jax.vjp(rms_norm, resid, gain_one)
     grad_resid_norm, gain_one_grad = norm_one_back(grad_normed)
     input_grad = grad_mixed + grad_resid_norm
-    fsdp_count = lax.axis_size("fsdp")
     own_expand = scatter_rows(full_expand, "fsdp")
     own_expand_rows = own_expand.shape[0]
     pieces = own_first.shape[0] // own_expand_rows

time: 1900 us -> 1690 us (0.89)
  Pallas kernels: 0 us -> 357 us
  blocking collectives: 273 us -> 6.61 us
  matrix products: 291 us -> 159 us
  waiting for transfers between devices: 799 us -> 738 us
  other arithmetic: 242 us -> 192 us
  local copies, waits for them, and re-layouts: 208 us -> 164 us
    pallas_call x0 -> x4, Pallas kernels: none -> 357 us  [the longest x1 149 us: experts_back(): pl.pallas_call(experts_back_kernel, in_specs=[any_spec()] * 5, out_specs=...]
    all_gather x6 -> x1, blocking collectives: 273 us -> 6.61 us  [per_device(): lax.all_gather(jnp.concatenate([attn_gain, ffn_gain, latent_gain, w_route...]
    all_to_all x4 -> x0, waiting for transfers between devices: 112 us -> none  [the longest x1 112 us: per_device(): lax.all_to_all(payload, ('replica', 'fsdp', 'ctx'), split_axis=0, concat_...]
    all_gather x1, waiting for transfers between devices: 0.01 us -> 64.4 us  [per_device(): lax.all_gather(shared_down, 'fsdp', axis=0, tiled=True)]
    dot_general x6 -> x0, matrix products: 57.7 us -> none  [the longest x1 14.3 us: per_device(): jnp.einsum('qhv,khv->hqk', grad_att, value_rows, preferred_element_type=j...]
    ppermute x44 -> x54, waiting for transfers between devices: 559 us -> 520 us  [swap(): return lax.ppermute(values, axis, [(i, i ^ mask) for i in range(count)])]
    all_gather x1, waiting for transfers between devices: 4.95 us -> 34.2 us  [per_device(): lax.all_gather(w_out, 'fsdp', axis=0, tiled=True)]
    dot_general x11 -> x8, matrix products: 86.3 us -> 58 us  [matmul(): return jnp.dot(first_mat, second_mat, preferred_element_type=jnp.float32)]
  transfers between devices with their start and end apart: 57 -> 63, of which waited for: 26 -> 33; matrix products, arithmetic and copies ran while one was open for 36% -> 27% of each run, Pallas kernels for 0% -> 21%
where the time goes in v2:
time: 1690 us; the launch traced here: 1680 us
  waiting for transfers between devices  738 us (44%)
  Pallas kernels  357 us (21%)
  other arithmetic  192 us (11%)
  local copies, waits for them, and re-layouts  164 us (10%)
  matrix products  159 us (9%)
  starting transfers between devices  43.2 us (3%)
  between operations  18.7 us (1%)
    ppermute x54, waiting for transfers between devices, swap(): return lax.ppermute(values, axis, [(i, i ^ mask) for i in range(count)])  520 us
    pallas_call x1, Pallas kernels, experts_back(): pl.pallas_call(experts_back_kernel, in_specs=[any_spec()] * 5, out_specs=...  149 us
    pallas_call x1, Pallas kernels, experts(): pl.pallas_call(experts_kernel, in_specs=[any_spec()] * 4, out_specs=(any_...  147 us
    all_gather x1, waiting for transfers between devices, per_device(): lax.all_gather(w_query, 'fsdp', axis=0, tiled=True)  72.3 us
    all_gather x1, waiting for transfers between devices, per_device(): lax.all_gather(shared_down, 'fsdp', axis=0, tiled=True)  64.4 us
    dot_general x8, matrix products, matmul(): return jnp.dot(first_mat, second_mat, preferred_element_type=jnp.float32)  58 us
    dot_general x9, matrix products, rows_dot(): lax.dot_general(first_mat, second_mat, (((0,), (0,)), ((), ())), preferre...  55.4 us
    dot_general x8, matrix products, cols_dot(): lax.dot_general(first_mat, second_mat, (((1,), (1,)), ((), ())), preferre...  45.5 us
  transfers between devices with their start and end apart: 63, of which 33 were waited for; matrix products, arithmetic and copies ran while one was open for 27% of the time, Pallas kernels for 21%

profile of v2, /device:TPU:0, one launch (start us, length us, event | category | flops | bytes accessed | tf_op | source)
XLA Modules:
  0.0 1679.2 jit_solution(6454377776392889682)
XLA Ops:
  9.7 6.6 all-gather.1
  19.5 16.9 %all-gather.13.cloned.1.call-done = bf16[2048,576]{0,1:T(8,128)(2,1)} async-done(((bf16[512,576]{0,1:T(8,128)(2,1)}), bf16[2048,576]{0,1:T(8,128)(2,1)}) %all-gather.13.cloned.1.call-update) | async-done | bytes 2359312 | tf_op jit(solution)/shard_map/all_gather | solution.py:647
  84.2 25.4 %all-gather.17.cloned.1.call-done = bf16[512,4096]{1,0:T(8,128)(2,1)} async-done(((bf16[128,4096]{1,0:T(8,128)(2,1)}), bf16[512,4096]{1,0:T(8,128)(2,1)}) %all-gather.17.cloned.1.call-update) | async-done | bytes 4194320 | tf_op jit(solution)/shard_map/all_gather | solution.py:648
  109.6 11.3 convolution_convert_fusion.e_ref
  120.9 72.3 %all-gather.11.cloned.1.call-done = bf16[2048,3072]{1,0:T(8,128)(2,1)} async-done(((bf16[512,3072]{1,0:T(8,128)(2,1)}), bf16[2048,3072]{1,0:T(8,128)(2,1)}) %all-gather.11.cloned.1.call-update) | async-done | bytes 12582928 | tf_op jit(solution)/shard_map/all_gather | solution.py:646
  193.1 6.6 fusion.107.q_ref
  200.1 16.9 %attention.1 = bf16[256,2048]{1,0:T(8,128)(2,1)S(1)} custom-call(f32[256,3072]{1,0:T(8,128)S(1)} %fusion.107.q_ref, bf16[1024,4096]{1,0:T(8,128)(2,1)S(1)} %copy-done, bf16[1024,64]{1,0:T(8,128)(2,1)S(1)} %slice.332.rope_ref, f32[256,32]{1,0:T(8,128)S(1)} %get-tuple-element.234.cos_ref, f32[256,32]{1,0:T(8,128)S(1)} %get-tuple-element.233.sin_ref, ...), custom_call_target="tpu_custom_call" | custom-call | flops 2684354560 | bytes 12582912 | tf_op jit(solution)/shard_map/attention/pallas_call | solution.py:208
  218.7 34.2 %all-gather.19.cloned.1.call-done = bf16[2048,2048]{1,0:T(8,128)(2,1)} async-done(((bf16[512,2048]{1,0:T(8,128)(2,1)}), bf16[2048,2048]{1,0:T(8,128)(2,1)}) %all-gather.19.cloned.1.call-update) | async-done | bytes 8388624 | tf_op jit(solution)/shard_map/all_gather | solution.py:649
  252.9 6.1 multiply_reduce_fusion.4
  271.0 147.1 %experts.1 = (bf16[32,40,2048]{2,1,0:T(8,128)(2,1)}, bf16[16,40,2048]{2,1,0:T(8,128)(2,1)}) custom-call(bf16[16,40,2048]{2,1,0:T(8,128)(2,1)} %broadcast_select_fusion.2.send, bf16[2048,704]{1,0:T(8,128)(2,1)} %bitcast.134, bf16[2048,704]{1,0:T(8,128)(2,1)} %bitcast.136, bf16[704,2048]{1,0:T(8,128)(2,1)} %bitcast.160), custom_call_target="tpu_custom_call" | custom-call | flops 11072962560 | bytes 419430400 | tf_op jit(solution)/shard_map/experts/pallas_call | solution.py:540
  422.9 7.9 gather_fusion.2
  435.3 6.0 reshape.373
  444.0 10.1 multiply_reduce_fusion.1
  454.1 9.1 fusion.109
  464.4 10.6 multiply_convert_fusion.2
  475.0 64.4 %all-gather.25.cloned.1.call-done = bf16[2816,2048]{1,0:T(8,128)(2,1)} async-done(((bf16[704,2048]{1,0:T(8,128)(2,1)}), bf16[2816,2048]{1,0:T(8,128)(2,1)}) %all-gather.25.cloned.1.call-update) | async-done | bytes 11534352 | tf_op jit(solution)/shard_map/all_gather | solution.py:682
  539.4 11.3 fusion.102
  558.4 6.0 mul.392
  580.5 148.8 %experts_back.1 = (bf16[32,40,2048]{2,1,0:T(8,128)(2,1)}, bf16[1280,704]{1,0:T(8,128)(2,1)}, bf16[1280,704]{1,0:T(8,128)(2,1)}, bf16[1280,704]{1,0:T(8,128)(2,1)}, bf16[16,40,2048]{2,1,0:T(8,128)(2,1)}) custom-call(bf16[16,40,2048]{2,1,0:T(8,128)(2,1)} %select_convert_fusion.1.send, bf16[32,40,2048]{2,1,0:T(8,128)(2,1)} %get-tuple-element.29.rows_in, ...), custom_call_target="tpu_custom_call" | custom-call | flops 18454937600 | bytes 419430400 | tf_op jit(solution)/shard_map/experts_back/pallas_call | solution.py:571
  734.1 7.9 gather_fusion.3
  746.5 6.2 reshape.375
  752.7 7.2 reduce_sum.190
  759.9 10.2 multiply_convert_fusion
  770.1 7.1 convolution_add_fusion.3
  777.3 6.4 convolution_add_fusion.2
  785.3 9.2 convolution_bitcast_fusion.2
  794.5 5.8 convolution_bitcast_fusion.1
  802.7 5.8 convolution_bitcast_fusion
  812.3 44.1 %attention_back.1 = (bf16[256,3072]{1,0:T(8,128)(2,1)S(1)}, bf16[1024,4096]{1,0:T(8,128)(2,1)}, f32[1024,64]{1,0:T(8,128)S(1)}) custom-call(f32[256,3072]{1,0:T(8,128)S(1)} %copy-done.2, bf16[1024,4096]{1,0:T(8,128)(2,1)} %convolution_convert_fusion.e_ref, bf16[1024,64]{1,0:T(8,128)(2,1)S(1)} %copy-done.4, f32[256,32]{1,0:T(8,128)S(1)} %copy-done.8, ...), custom_call_target="tpu_custom_call" | custom-call | flops 6979321856 | bytes 25165824 | tf_op jit(solution)/shard_map/attention_back/pallas_call | solution.py:244
  856.4 8.3 fusion.111
  893.4 19.2 %collective-permute-done.44 = bf16[256,1408]{1,0:T(8,128)(2,1)} collective-permute-done((bf16[256,1408]{1,0:T(8,128)(2,1)}, bf16[256,1408]{1,0:T(8,128)(2,1)}, u32[]{:S(2)}, u32[]{:S(2)}) %collective-permute-start.44) | collective-permute-done | bytes 720928 | tf_op jit(solution)/shard_map/ppermute | solution.py:63
  920.3 48.5 %collective-permute-done.24 = bf16[256,1024]{1,0:T(8,128)(2,1)} collective-permute-done((bf16[256,1024]{1,0:T(8,128)(2,1)}, bf16[256,1024]{1,0:T(8,128)(2,1)}, u32[]{:S(2)}, u32[]{:S(2)}) %collective-permute-start.24) | collective-permute-done | bytes 524320 | tf_op jit(solution)/shard_map/ppermute | solution.py:63
  971.1 8.0 collective-permute-done.34
  990.5 5.3 convert_add_fusion.3
  1013.3 39.0 %collective-permute-done.16 = bf16[1024,19]{1,0:T(8,128)(2,1)S(1)} collective-permute-done((bf16[1024,19]{1,0:T(8,128)(2,1)S(1)}, bf16[1024,19]{1,0:T(8,128)(2,1)S(1)}, u32[]{:S(2)}, u32[]{:S(2)}) %collective-permute-start.16) | collective-permute-done | bytes 38944 | tf_op jit(solution)/shard_map/ppermute | solution.py:63
  1058.1 5.7 pad_maximum_fusion
  1080.9 15.3 collective-permute-done.28
  1099.5 7.6 collective-permute-done.12
  1115.9 6.1 copy.208
  1122.0 7.7 collective-permute-done.48
  1136.4 15.9 collective-permute-done.49
  1154.9 11.5 collective-permute-done.30
  1166.5 17.8 %collective-permute-done.50 = bf16[88,2048]{1,0:T(8,128)(2,1)S(1)} collective-permute-done((bf16[88,2048]{1,0:T(8,128)(2,1)S(1)}, bf16[88,2048]{1,0:T(8,128)(2,1)S(1)}, u32[]{:S(2)}, u32[]{:S(2)}) %collective-permute-start.50) | collective-permute-done | bytes 360480 | tf_op jit(solution)/shard_map/ppermute | solution.py:63
  1184.5 14.2 collective-permute-done.31
  1198.8 17.8 %collective-permute-done.51 = bf16[88,2048]{1,0:T(8,128)(2,1)S(1)} collective-permute-done((bf16[88,2048]{1,0:T(8,128)(2,1)S(1)}, bf16[88,2048]{1,0:T(8,128)(2,1)S(1)}, u32[]{:S(2)}, u32[]{:S(2)}) %collective-permute-start.51) | collective-permute-done | bytes 360480 | tf_op jit(solution)/shard_map/ppermute | solution.py:63
  1216.7 13.7 collective-permute-done.32
  1232.1 15.6 collective-permute-done.52
  1249.3 9.2 fusion.8
  1258.5 10.9 concatenate.147
  1278.0 10.3 fusion
  1297.9 33.9 %collective-permute-done.18 = bf16[256,4691]{0,1:T(8,128)(2,1)} collective-permute-done((bf16[256,4691]{0,1:T(8,128)(2,1)}, bf16[256,4691]{0,1:T(8,128)(2,1)}, u32[]{:S(2)}, u32[]{:S(2)}) %collective-permute-start.18) | collective-permute-done | bytes 2401824 | tf_op jit(solution)/shard_map/ppermute | solution.py:63
  1343.7 49.8 %collective-permute-done.38 = bf16[256,5632]{1,0:T(8,128)(2,1)} collective-permute-done((bf16[256,5632]{1,0:T(8,128)(2,1)}, bf16[256,5632]{1,0:T(8,128)(2,1)}, u32[]{:S(2)}, u32[]{:S(2)}) %collective-permute-start.38) | collective-permute-done | bytes 2883616 | tf_op jit(solution)/shard_map/ppermute | solution.py:63
  1393.5 8.9 convert_add_fusion
  1414.1 17.0 %collective-permute-done.20 = bf16[64,4691]{1,0:T(8,128)(2,1)S(1)} collective-permute-done((bf16[64,4691]{1,0:T(8,128)(2,1)S(1)}, bf16[64,4691]{1,0:T(8,128)(2,1)S(1)}, u32[]{:S(2)}, u32[]{:S(2)}) %collective-permute-start.20) | collective-permute-done | bytes 600480 | tf_op jit(solution)/shard_map/ppermute | solution.py:63
  1431.4 31.3 %collective-permute-done.39 = bf16[128,5632]{1,0:T(8,128)(2,1)S(1)} collective-permute-done((bf16[128,5632]{1,0:T(8,128)(2,1)S(1)}, bf16[128,5632]{1,0:T(8,128)(2,1)S(1)}, u32[]{:S(2)}, u32[]{:S(2)}) %collective-permute-start.39) | collective-permute-done | bytes 1441824 | tf_op jit(solution)/shard_map/ppermute | solution.py:63
  1472.8 20.9 %collective-permute-done.40 = bf16[64,5632]{1,0:T(8,128)(2,1)} collective-permute-done((bf16[64,5632]{1,0:T(8,128)(2,1)}, bf16[64,5632]{1,0:T(8,128)(2,1)}, u32[]{:S(2)}, u32[]{:S(2)}) %collective-permute-start.40) | collective-permute-done | bytes 720928 | tf_op jit(solution)/shard_map/ppermute | solution.py:63
  1502.2 11.0 collective-permute-done.22
  1514.9 15.6 collective-permute-done.41
  1539.4 5.2 maximum_convert_fusion.2
  1544.6 21.9 %collective-permute-done.42 = bf16[128,5632]{1,0:T(8,128)(2,1)} collective-permute-done((bf16[128,5632]{1,0:T(8,128)(2,1)}, bf16[128,5632]{1,0:T(8,128)(2,1)}, u32[]{:S(2)}, u32[]{:S(2)}) %collective-permute-start.42) | collective-permute-done | bytes 1441824 | tf_op jit(solution)/shard_map/ppermute | solution.py:63
  1572.5 20.7 %collective-permute-done.23 = bf16[256,4691]{0,1:T(8,128)(2,1)S(1)} collective-permute-done((bf16[256,4691]{0,1:T(8,128)(2,1)}, bf16[256,4691]{0,1:T(8,128)(2,1)S(1)}, u32[]{:S(2)}, u32[]{:S(2)}) %collective-permute-start.23) | collective-permute-done | bytes 2401824 | tf_op jit(solution)/shard_map/ppermute | solution.py:63
  1613.3 40.4 %collective-permute-done.43 = bf16[256,5632]{1,0:T(8,128)(2,1)} collective-permute-done((bf16[256,5632]{1,0:T(8,128)(2,1)}, bf16[256,5632]{1,0:T(8,128)(2,1)}, u32[]{:S(2)}, u32[]{:S(2)}) %collective-permute-start.43) | collective-permute-done | bytes 2883616 | tf_op jit(solution)/shard_map/ppermute | solution.py:63
  1656.1 5.8 maximum_convert_fusion
  1661.8 9.5 fusion.104
  (561 shorter events, 333.8 us)
Async XLA Ops:
  7.2 29.2 %all-gather.13.cloned.1.call-start = ((), (), s32[]{:S(2)}) async-start(), calls=%async_computation.2 | async-start | bytes 2949120 | tf_op jit(solution)/shard_map/all_gather | solution.py:647
  7.9 75.2 %all-gather.15.cloned.1.call-start = ((), (), s32[]{:S(2)}) async-start(), calls=%async_computation.3 | async-start | bytes 1638400 | tf_op jit(solution)/shard_map/all_gather | solution.py:670
  40.6 159.1 %copy-start.5 = (f32[256,32]{1,0:T(8,128)}, f32[256,32]{1,0:T(8,128)S(1)}, u32[]{:S(2)}) copy-start(f32[256,32]{1,0:T(8,128)S(1)} %get-tuple-element.233.sin_ref) | copy-start | bytes 98308
  41.4 68.1 %all-gather.17.cloned.1.call-start = ((), (), s32[]{:S(2)}) async-start(), calls=%async_computation.4 | async-start | bytes 5242880 | tf_op jit(solution)/shard_map/all_gather | solution.py:648
  42.2 150.9 %all-gather.11.cloned.1.call-start = ((), (), s32[]{:S(2)}) async-start(), calls=%async_computation.1 | async-start | bytes 15728640 | tf_op jit(solution)/shard_map/all_gather | solution.py:646
  42.8 210.1 %all-gather.19.cloned.1.call-start = ((), (), s32[]{:S(2)}) async-start(), calls=%async_computation.5 | async-start | bytes 10485760 | tf_op jit(solution)/shard_map/all_gather | solution.py:649
  43.4 410.8 %all-gather.21.cloned.1.call-start = ((), (), s32[]{:S(2)}) async-start(), calls=%async_computation.6 | async-start | bytes 14417920 | tf_op jit(solution)/shard_map/all_gather | solution.py:680
  44.0 420.4 %all-gather.23.cloned.1.call-start = ((), (), s32[]{:S(2)}) async-start(), calls=%async_computation.7 | async-start | bytes 14417920 | tf_op jit(solution)/shard_map/all_gather | solution.py:681
  44.7 494.6 %all-gather.25.cloned.1.call-start = ((), (), s32[]{:S(2)}) async-start(), calls=%async_computation.8 | async-start | bytes 14417920 | tf_op jit(solution)/shard_map/all_gather | solution.py:682
  45.5 953.5 %reduce-scatter.2.cloned.1.call-start = ((), (), s32[]{:S(2)}) async-start(), calls=%async_computation.9 | async-start | bytes 1638400 | tf_op jit(solution)/shard_map/reduce_scatter | solution.py:786
  46.8 10.2 collective-permute-start.5
  48.0 34.0 %collective-permute-start.10 = (bf16[256,1024]{1,0:T(8,128)(2,1)}, bf16[256,1024]{1,0:T(8,128)(2,1)S(1)}, u32[]{:S(2)}, u32[]{:S(2)}) collective-permute-start(bf16[256,1024]{1,0:T(8,128)(2,1)} %get-tuple-element.220), channel_id=1, source_target_pairs={{0,8},{4,12},{8,0},{12,4},{1,9},{5,13},{9,1},{13,5},{2,10},{6,14},... | collective-permute-start | bytes 1572872 | tf_op jit(solution)/shard_map/ppermute | solution.py:63
  57.7 1.2 collective-permute-start.6
  59.6 3.7 collective-permute-start.7
  63.3 4.7 collective-permute-start.8
  67.9 12.8 collective-permute-start.9
  551.9 314.6 %collective-permute-start = (f32[8,128]{1,0:T(8,128)}, f32[8,128]{1,0:T(8,128)}, u32[]{:S(2)}, u32[]{:S(2)}) collective-permute-start(f32[8,128]{1,0:T(8,128)} %broadcast_in_dim.138), channel_id=1, source_target_pairs={{0,8},{4,12},{8,0},{12,4},{1,9},{5,13},{9,1},{13,5},{2,10},{6,14},... | collective-permute-start | bytes 12296 | tf_op jit(solution)/shard_map/ppermute | solution.py:63
  552.2 429.3 %collective-permute-start.46 = (bf16[256,2048]{1,0:T(8,128)(2,1)}, bf16[256,2048]{1,0:T(8,128)(2,1)}, u32[]{:S(2)}, u32[]{:S(2)}) collective-permute-start(bf16[256,2048]{1,0:T(8,128)(2,1)} %get-tuple-element.167), channel_id=1, source_target_pairs={{0,8},{4,12},{8,0},{12,4},{1,9},{5,13},{9,1},{13,5},{2,10},{6,14},... | collective-permute-start | bytes 3145736 | tf_op jit(solution)/shard_map/ppermute | solution.py:63
  867.9 4.9 collective-permute-start.1
  870.8 114.8 %collective-permute-start.26 = (bf16[256,2048]{1,0:T(8,128)(2,1)}, bf16[256,2048]{1,0:T(8,128)(2,1)}, u32[]{:S(2)}, u32[]{:S(2)}) collective-permute-start(bf16[256,2048]{1,0:T(8,128)(2,1)} %get-tuple-element.165), channel_id=1, source_target_pairs={{0,8},{4,12},{8,0},{12,4},{1,9},{5,13},{9,1},{13,5},{2,10},{6,14},... | collective-permute-start | bytes 3145736 | tf_op jit(solution)/shard_map/ppermute | solution.py:63
  871.8 40.8 %collective-permute-start.44 = (bf16[256,1408]{1,0:T(8,128)(2,1)}, bf16[256,1408]{1,0:T(8,128)(2,1)}, u32[]{:S(2)}, u32[]{:S(2)}) collective-permute-start(bf16[256,1408]{1,0:T(8,128)(2,1)} %get-tuple-element.202), channel_id=1, source_target_pairs={{0,8},{4,12},{8,0},{12,4},{1,9},{5,13},{9,1},{13,5},{2,10},{6,14},... | collective-permute-start | bytes 2162696 | tf_op jit(solution)/shard_map/ppermute | solution.py:63
  874.2 5.4 collective-permute-start.2
  879.6 6.8 collective-permute-start.3
  885.5 104.9 %collective-permute-start.14 = (bf16[256,4096]{1,0:T(8,128)(2,1)}, bf16[256,4096]{1,0:T(8,128)(2,1)}, u32[]{:S(2)}, u32[]{:S(2)}) collective-permute-start(bf16[256,4096]{1,0:T(8,128)(2,1)} %select_convert_fusion.3), channel_id=1, source_target_pairs={{0,8},{4,12},{8,0},{12,4},{1,9},{5,13},{9,1},{13,5},{2,10},{6,14},... | collective-permute-start | bytes 6291464 | tf_op jit(solution)/shard_map/ppermute | solution.py:63
  886.4 4.6 collective-permute-start.4
  891.0 77.7 %collective-permute-start.24 = (bf16[256,1024]{1,0:T(8,128)(2,1)}, bf16[256,1024]{1,0:T(8,128)(2,1)}, u32[]{:S(2)}, u32[]{:S(2)}) collective-permute-start(bf16[256,1024]{1,0:T(8,128)(2,1)} %get-tuple-element.216), channel_id=1, source_target_pairs={{0,8},{4,12},{8,0},{12,4},{1,9},{5,13},{9,1},{13,5},{2,10},{6,14},... | collective-permute-start | bytes 1572872 | tf_op jit(solution)/shard_map/ppermute | solution.py:63
  912.6 66.5 %collective-permute-start.34 = (bf16[256,1024]{1,0:T(8,128)(2,1)}, bf16[256,1024]{1,0:T(8,128)(2,1)}, u32[]{:S(2)}, u32[]{:S(2)}) collective-permute-start(bf16[256,1024]{1,0:T(8,128)(2,1)} %get-tuple-element.210), channel_id=1, source_target_pairs={{0,8},{4,12},{8,0},{12,4},{1,9},{5,13},{9,1},{13,5},{2,10},{6,14},... | collective-permute-start | bytes 1572872 | tf_op jit(solution)/shard_map/ppermute | solution.py:63
  968.8 20.2 %collective-permute-start.45 = (bf16[512,704]{0,1:T(8,128)(2,1)}, bf16[512,704]{0,1:T(8,128)(2,1)S(1)}, u32[]{:S(2)}, u32[]{:S(2)}) collective-permute-start(bf16[512,704]{0,1:T(8,128)(2,1)} %copy.223), channel_id=1, source_target_pairs={{0,4},{4,0},{8,12},{12,8},{1,5},{5,1},{9,13},{13,9},{2,6},{6,2},{1... | collective-permute-start | bytes 2162696 | tf_op jit(solution)/shard_map/ppermute | solution.py:63
  979.1 270.2 %collective-permute-start.11 = (bf16[512,512]{1,0:T(8,128)(2,1)}, bf16[512,512]{1,0:T(8,128)(2,1)}, u32[]{:S(2)}, u32[]{:S(2)}) collective-permute-start(bf16[512,512]{1,0:T(8,128)(2,1)} %get-tuple-element.218), channel_id=1, source_target_pairs={{0,4},{4,0},{8,12},{12,8},{1,5},{5,1},{9,13},{13,9},{2,6},{6,2},{1... | collective-permute-start | bytes 1572872 | tf_op jit(solution)/shard_map/ppermute | solution.py:63
  981.6 76.5 %collective-permute-start.36 = (bf16[256,5632]{1,0:T(8,128)(2,1)}, bf16[256,5632]{1,0:T(8,128)(2,1)}, u32[]{:S(2)}, u32[]{:S(2)}) collective-permute-start(bf16[256,5632]{1,0:T(8,128)(2,1)} %pad_maximum_fusion.2), channel_id=1, source_target_pairs={{0,8},{4,12},{8,0},{12,4},{1,9},{5,13},{9,1},{13,5},{2,10},{6,14},... | collective-permute-start | bytes 8650760 | tf_op jit(solution)/shard_map/ppermute | solution.py:63
  985.6 78.2 %collective-permute-start.25 = (bf16[512,512]{1,0:T(8,128)(2,1)}, bf16[512,512]{1,0:T(8,128)(2,1)}, u32[]{:S(2)}, u32[]{:S(2)}) collective-permute-start(bf16[512,512]{1,0:T(8,128)(2,1)} %get-tuple-element.214), channel_id=1, source_target_pairs={{0,4},{4,0},{8,12},{12,8},{1,5},{5,1},{9,13},{13,9},{2,6},{6,2},{1... | collective-permute-start | bytes 1572872 | tf_op jit(solution)/shard_map/ppermute | solution.py:63
  989.0 75.3 %collective-permute-start.27 = (bf16[512,2048]{1,0:T(8,128)(2,1)}, bf16[512,2048]{1,0:T(8,128)(2,1)}, u32[]{:S(2)}, u32[]{:S(2)}) collective-permute-start(bf16[512,2048]{1,0:T(8,128)(2,1)} %pad_maximum_fusion.7), channel_id=1, source_target_pairs={{0,4},{4,0},{8,12},{12,8},{1,5},{5,1},{9,13},{13,9},{2,6},{6,2},{1... | collective-permute-start | bytes 6291464 | tf_op jit(solution)/shard_map/ppermute | solution.py:63
  1007.0 45.3 %collective-permute-start.16 = (bf16[1024,19]{1,0:T(8,128)(2,1)S(1)}, bf16[1024,19]{1,0:T(8,128)(2,1)S(1)}, u32[]{:S(2)}, u32[]{:S(2)}) collective-permute-start(bf16[1024,19]{1,0:T(8,128)(2,1)S(1)} %select_convert_fusion.15), channel_id=1, source_target_pairs={{0,8},{4,12},{8,0},{12,4},{1,9},{5,13},{9,1},{13,5},{2,10},{6,14},... | collective-permute-start | bytes 116744 | tf_op jit(solution)/shard_map/ppermute | solution.py:63
  1053.2 2.5 collective-permute-start.17
  1055.7 14.8 collective-permute-start.47
  1058.0 12.1 collective-permute-start.15
  1063.8 214.1 %collective-permute-start.35 = (bf16[512,512]{1,0:T(8,128)(2,1)}, bf16[512,512]{1,0:T(8,128)(2,1)}, u32[]{:S(2)}, u32[]{:S(2)}) collective-permute-start(bf16[512,512]{1,0:T(8,128)(2,1)} %get-tuple-element.208), channel_id=1, source_target_pairs={{0,4},{4,0},{8,12},{12,8},{1,5},{5,1},{9,13},{13,9},{2,6},{6,2},{1... | collective-permute-start | bytes 1572872 | tf_op jit(solution)/shard_map/ppermute | solution.py:63
  1064.3 42.7 %collective-permute-start.12 = (bf16[256,3648]{0,1:T(8,128)(2,1)S(1)}, bf16[256,3648]{0,1:T(8,128)(2,1)S(1)}, u32[]{:S(2)}, u32[]{:S(2)}) collective-permute-start(bf16[256,3648]{0,1:T(8,128)(2,1)S(1)} %copy-done.71), channel_id=1, source_target_pairs={{0,8},{4,12},{8,0},{12,4},{1,9},{5,13},{9,1},{13,5},{2,10},{6,14},... | collective-permute-start | bytes 5603336 | tf_op jit(solution)/shard_map/ppermute | solution.py:63
  1070.1 207.8 %collective-permute-start.37 = (bf16[512,5632]{1,0:T(8,128)(2,1)}, bf16[512,5632]{1,0:T(8,128)(2,1)}, u32[]{:S(2)}, u32[]{:S(2)}) collective-permute-start(bf16[512,5632]{1,0:T(8,128)(2,1)} %pad_maximum_fusion), channel_id=1, source_target_pairs={{0,4},{4,0},{8,12},{12,8},{1,5},{5,1},{9,13},{13,9},{2,6},{6,2},{1... | collective-permute-start | bytes 17301512 | tf_op jit(solution)/shard_map/ppermute | solution.py:63
  1070.5 25.6 %collective-permute-start.28 = (bf16[256,2048]{1,0:T(8,128)(2,1)S(1)}, bf16[256,2048]{1,0:T(8,128)(2,1)S(1)}, u32[]{:S(2)}, u32[]{:S(2)}) collective-permute-start(bf16[256,2048]{1,0:T(8,128)(2,1)S(1)} %select_convert_fusion.7), channel_id=1, source_target_pairs={{0,16},{16,0},{1,17},{17,1},{2,18},{18,2},{3,19},{19,3},{4,20},{20... | collective-permute-start | bytes 3145736 | tf_op jit(solution)/shard_map/ppermute | solution.py:63
  1096.2 33.5 %collective-permute-start.48 = (bf16[352,2048]{1,0:T(8,128)(2,1)}, bf16[352,2048]{1,0:T(8,128)(2,1)}, u32[]{:S(2)}, u32[]{:S(2)}) collective-permute-start(bf16[352,2048]{1,0:T(8,128)(2,1)} %select_convert_fusion.4), channel_id=1, source_target_pairs={{0,16},{16,0},{1,17},{17,1},{2,18},{18,2},{3,19},{19,3},{4,20},{20... | collective-permute-start | bytes 4325384 | tf_op jit(solution)/shard_map/ppermute | solution.py:63
  1108.3 25.4 %collective-permute-start.29 = (bf16[128,2048]{1,0:T(8,128)(2,1)}, bf16[128,2048]{1,0:T(8,128)(2,1)}, u32[]{:S(2)}, u32[]{:S(2)}) collective-permute-start(bf16[128,2048]{1,0:T(8,128)(2,1)} %select_convert_fusion.12), channel_id=1, source_target_pairs={{0,1},{1,0},{2,3},{3,2},{4,5},{5,4},{6,7},{7,6},{8,9},{9,8},{10,11... | collective-permute-start | bytes 1572872 | tf_op jit(solution)/shard_map/ppermute | solution.py:63
  1129.7 119.6 %collective-permute-start.13 = (bf16[512,3648]{0,1:T(8,128)(2,1)}, bf16[512,3648]{0,1:T(8,128)(2,1)S(1)}, u32[]{:S(2)}, u32[]{:S(2)}) collective-permute-start(bf16[512,3648]{0,1:T(8,128)(2,1)} %copy.208), channel_id=1, source_target_pairs={{0,4},{4,0},{8,12},{12,8},{1,5},{5,1},{9,13},{13,9},{2,6},{6,2},{1... | collective-permute-start | bytes 11206664 | tf_op jit(solution)/shard_map/ppermute | solution.py:63
  1133.7 18.6 %collective-permute-start.49 = (bf16[176,2048]{1,0:T(8,128)(2,1)S(1)}, bf16[176,2048]{1,0:T(8,128)(2,1)S(1)}, u32[]{:S(2)}, u32[]{:S(2)}) collective-permute-start(bf16[176,2048]{1,0:T(8,128)(2,1)S(1)} %select_convert_fusion.9), channel_id=1, source_target_pairs={{0,1},{1,0},{2,3},{3,2},{4,5},{5,4},{6,7},{7,6},{8,9},{9,8},{10,11... | collective-permute-start | bytes 2162696 | tf_op jit(solution)/shard_map/ppermute | solution.py:63
  1152.3 14.2 collective-permute-start.30
  1166.5 17.9 %collective-permute-start.50 = (bf16[88,2048]{1,0:T(8,128)(2,1)S(1)}, bf16[88,2048]{1,0:T(8,128)(2,1)S(1)}, u32[]{:S(2)}, u32[]{:S(2)}) collective-permute-start(bf16[88,2048]{1,0:T(8,128)(2,1)S(1)} %select_convert_fusion.13), channel_id=1, source_target_pairs={{0,2},{1,3},{2,0},{3,1},{4,6},{5,7},{6,4},{7,5},{8,10},{9,11},{10,... | collective-permute-start | bytes 1081352 | tf_op jit(solution)/shard_map/ppermute | solution.py:63
  1184.3 14.4 collective-permute-start.31
  1198.7 17.9 %collective-permute-start.51 = (bf16[88,2048]{1,0:T(8,128)(2,1)S(1)}, bf16[88,2048]{1,0:T(8,128)(2,1)S(1)}, u32[]{:S(2)}, u32[]{:S(2)}) collective-permute-start(bf16[88,2048]{1,0:T(8,128)(2,1)S(1)} %add_convert_fusion.2), channel_id=1, source_target_pairs={{0,2},{1,3},{2,0},{3,1},{4,6},{5,7},{6,4},{7,5},{8,10},{9,11},{10,... | collective-permute-start | bytes 1081352 | tf_op jit(solution)/shard_map/ppermute | solution.py:63
  1216.6 13.9 collective-permute-start.32
  1230.4 17.2 %collective-permute-start.52 = (bf16[176,2048]{1,0:T(8,128)(2,1)S(1)}, bf16[176,2048]{1,0:T(8,128)(2,1)S(1)}, u32[]{:S(2)}, u32[]{:S(2)}) collective-permute-start(bf16[176,2048]{1,0:T(8,128)(2,1)S(1)} %pad_maximum_fusion.16), channel_id=1, source_target_pairs={{0,1},{1,0},{2,3},{3,2},{4,5},{5,4},{6,7},{7,6},{8,9},{9,8},{10,11... | collective-permute-start | bytes 2162696 | tf_op jit(solution)/shard_map/ppermute | solution.py:63
  1247.7 163.4 %collective-permute-start.33 = (bf16[256,2048]{1,0:T(8,128)(2,1)}, bf16[256,2048]{1,0:T(8,128)(2,1)}, u32[]{:S(2)}, u32[]{:S(2)}) collective-permute-start(bf16[256,2048]{1,0:T(8,128)(2,1)} %pad_maximum_fusion.14), channel_id=1, source_target_pairs={{0,16},{16,0},{1,17},{17,1},{2,18},{18,2},{3,19},{19,3},{4,20},{20... | collective-permute-start | bytes 3145736 | tf_op jit(solution)/shard_map/ppermute | solution.py:63
  1276.3 55.5 %collective-permute-start.18 = (bf16[256,4691]{0,1:T(8,128)(2,1)}, bf16[256,4691]{0,1:T(8,128)(2,1)}, u32[]{:S(2)}, u32[]{:S(2)}) collective-permute-start(bf16[256,4691]{0,1:T(8,128)(2,1)} %copy.213), channel_id=1, source_target_pairs={{0,16},{16,0},{1,17},{17,1},{2,18},{18,2},{3,19},{19,3},{4,20},{20... | collective-permute-start | bytes 7205384 | tf_op jit(solution)/shard_map/ppermute | solution.py:63
  1294.6 98.9 %collective-permute-start.38 = (bf16[256,5632]{1,0:T(8,128)(2,1)}, bf16[256,5632]{1,0:T(8,128)(2,1)}, u32[]{:S(2)}, u32[]{:S(2)}) collective-permute-start(bf16[256,5632]{1,0:T(8,128)(2,1)} %select_convert_fusion), channel_id=1, source_target_pairs={{0,16},{16,0},{1,17},{17,1},{2,18},{18,2},{3,19},{19,3},{4,20},{20... | collective-permute-start | bytes 8650760 | tf_op jit(solution)/shard_map/ppermute | solution.py:63
  1296.2 202.3 %collective-permute-start.53 = (bf16[352,2048]{1,0:T(8,128)(2,1)}, bf16[352,2048]{1,0:T(8,128)(2,1)}, u32[]{:S(2)}, u32[]{:S(2)}) collective-permute-start(bf16[352,2048]{1,0:T(8,128)(2,1)} %pad_maximum_fusion.11), channel_id=1, source_target_pairs={{0,16},{16,0},{1,17},{17,1},{2,18},{18,2},{3,19},{19,3},{4,20},{20... | collective-permute-start | bytes 4325384 | tf_op jit(solution)/shard_map/ppermute | solution.py:63
  1343.1 59.4 %collective-permute-start.19 = (bf16[128,4691]{0,1:T(8,128)(2,1)S(1)}, bf16[128,4691]{0,1:T(8,128)(2,1)}, u32[]{:S(2)}, u32[]{:S(2)}) collective-permute-start(bf16[128,4691]{0,1:T(8,128)(2,1)S(1)} %copy.215), channel_id=1, source_target_pairs={{0,1},{1,0},{2,3},{3,2},{4,5},{5,4},{6,7},{7,6},{8,9},{9,8},{10,11... | collective-permute-start | bytes 3602696 | tf_op jit(solution)/shard_map/ppermute | solution.py:63
  1407.5 23.6 %collective-permute-start.20 = (bf16[64,4691]{1,0:T(8,128)(2,1)S(1)}, bf16[64,4691]{1,0:T(8,128)(2,1)S(1)}, u32[]{:S(2)}, u32[]{:S(2)}) collective-permute-start(bf16[64,4691]{1,0:T(8,128)(2,1)S(1)} %select_convert_fusion.11), channel_id=1, source_target_pairs={{0,2},{1,3},{2,0},{3,1},{4,6},{5,7},{6,4},{7,5},{8,10},{9,11},{10,... | collective-permute-start | bytes 1801352 | tf_op jit(solution)/shard_map/ppermute | solution.py:63
  1409.6 53.1 %collective-permute-start.39 = (bf16[128,5632]{1,0:T(8,128)(2,1)S(1)}, bf16[128,5632]{1,0:T(8,128)(2,1)S(1)}, u32[]{:S(2)}, u32[]{:S(2)}) collective-permute-start(bf16[128,5632]{1,0:T(8,128)(2,1)S(1)} %select_convert_fusion.5), channel_id=1, source_target_pairs={{0,1},{1,0},{2,3},{3,2},{4,5},{5,4},{6,7},{7,6},{8,9},{9,8},{10,11... | collective-permute-start | bytes 4325384 | tf_op jit(solution)/shard_map/ppermute | solution.py:63
  1431.3 34.4 %collective-permute-start.21 = (bf16[64,4691]{1,0:T(8,128)(2,1)S(1)}, bf16[64,4691]{1,0:T(8,128)(2,1)S(1)}, u32[]{:S(2)}, u32[]{:S(2)}) collective-permute-start(bf16[64,4691]{1,0:T(8,128)(2,1)S(1)} %add_convert_fusion.1), channel_id=1, source_target_pairs={{0,2},{1,3},{2,0},{3,1},{4,6},{5,7},{6,4},{7,5},{8,10},{9,11},{10,... | collective-permute-start | bytes 1801352 | tf_op jit(solution)/shard_map/ppermute | solution.py:63
  1465.7 28.0 %collective-permute-start.40 = (bf16[64,5632]{1,0:T(8,128)(2,1)}, bf16[64,5632]{1,0:T(8,128)(2,1)}, u32[]{:S(2)}, u32[]{:S(2)}) collective-permute-start(bf16[64,5632]{1,0:T(8,128)(2,1)} %select_convert_fusion.10), channel_id=1, source_target_pairs={{0,2},{1,3},{2,0},{3,1},{4,6},{5,7},{6,4},{7,5},{8,10},{9,11},{10,... | collective-permute-start | bytes 2162696 | tf_op jit(solution)/shard_map/ppermute | solution.py:63
  1470.4 42.7 %collective-permute-start.22 = (bf16[128,4691]{0,1:T(8,128)(2,1)}, bf16[128,4691]{0,1:T(8,128)(2,1)}, u32[]{:S(2)}, u32[]{:S(2)}) collective-permute-start(bf16[128,4691]{0,1:T(8,128)(2,1)} %copy.217), channel_id=1, source_target_pairs={{0,1},{1,0},{2,3},{3,2},{4,5},{5,4},{6,7},{7,6},{8,9},{9,8},{10,11... | collective-permute-start | bytes 3602696 | tf_op jit(solution)/shard_map/ppermute | solution.py:63
  1495.9 34.6 %collective-permute-start.41 = (bf16[64,5632]{1,0:T(8,128)(2,1)}, bf16[64,5632]{1,0:T(8,128)(2,1)S(1)}, u32[]{:S(2)}, u32[]{:S(2)}) collective-permute-start(bf16[64,5632]{1,0:T(8,128)(2,1)} %add_convert_fusion), channel_id=1, source_target_pairs={{0,2},{1,3},{2,0},{3,1},{4,6},{5,7},{6,4},{7,5},{8,10},{9,11},{10,... | collective-permute-start | bytes 2162696 | tf_op jit(solution)/shard_map/ppermute | solution.py:63
  1533.1 33.4 %collective-permute-start.42 = (bf16[128,5632]{1,0:T(8,128)(2,1)}, bf16[128,5632]{1,0:T(8,128)(2,1)}, u32[]{:S(2)}, u32[]{:S(2)}) collective-permute-start(bf16[128,5632]{1,0:T(8,128)(2,1)} %pad_maximum_fusion.10), channel_id=1, source_target_pairs={{0,1},{1,0},{2,3},{3,2},{4,5},{5,4},{6,7},{7,6},{8,9},{9,8},{10,11... | collective-permute-start | bytes 4325384 | tf_op jit(solution)/shard_map/ppermute | solution.py:63
  1537.9 55.3 %collective-permute-start.23 = (bf16[256,4691]{0,1:T(8,128)(2,1)}, bf16[256,4691]{0,1:T(8,128)(2,1)S(1)}, u32[]{:S(2)}, u32[]{:S(2)}) collective-permute-start(bf16[256,4691]{0,1:T(8,128)(2,1)} %copy.220), channel_id=1, source_target_pairs={{0,16},{16,0},{1,17},{17,1},{2,18},{18,2},{3,19},{19,3},{4,20},{20... | collective-permute-start | bytes 7205384 | tf_op jit(solution)/shard_map/ppermute | solution.py:63
  1570.9 82.8 %collective-permute-start.43 = (bf16[256,5632]{1,0:T(8,128)(2,1)}, bf16[256,5632]{1,0:T(8,128)(2,1)}, u32[]{:S(2)}, u32[]{:S(2)}) collective-permute-start(bf16[256,5632]{1,0:T(8,128)(2,1)} %pad_maximum_fusion.3), channel_id=1, source_target_pairs={{0,16},{16,0},{1,17},{17,1},{2,18},{18,2},{3,19},{19,3},{4,20},{20... | collective-permute-start | bytes 8650760 | tf_op jit(solution)/shard_map/ppermute | solution.py:63
  (117 other events, 1654.1 us)
Sparse Core Ops, SparseCore 0:
  9.6 26.7 all-gather.12
  41.6 32.8 all-gather.14
  76.0 33.4 all-gather.16
  111.0 82.0 all-gather.10
  194.5 58.2 all-gather.18
  254.3 104.2 all-gather.20
  360.1 104.2 all-gather.22
  465.9 73.3 all-gather.24
  893.5 31.4 reduce-scatter.1
